TPU v7x, 512 devices: a whole 4x8x8 slice. The times are simulated.
512 devices in a mesh: blk: 64 (over x, y, z_hi), uly: 8 (over z_lo, core).
Axes of the slice: x: 4, y: 8, z: 8 (z_hi: 2, z_lo: 4; z = z_hi * 4 + z_lo), core: 2. Of those that a mesh axis runs over, the one named last changes fastest.
Arguments:
- residual: bfloat16 [6144, 2048], P(('blk', 'uly')), may hold values from -24 to 24
- query_projection: bfloat16 [6144, 4096], P(('blk', 'uly')), may hold values from -51 to 51
- key_projection: bfloat16 [6144, 1024], P(('blk', 'uly')), may hold values from -5.1 to 5.1
- value_projection: bfloat16 [6144, 1024], P(('blk', 'uly')), may hold values from -6 to 6
- gate_proj: bfloat16 [6144, 4096], P(('blk', 'uly')), may hold values from -6 to 6
- positions: int32 [6144], replicated, may hold values from 0 to 6143, each once
- prefix_len: int32 [1], replicated, may hold values from 768 to 3071
- out_weight: bfloat16 [4096, 2048], P('uly', 'blk'), may hold values from -0.375 to 0.375
- norm_gain: float32 [2048], replicated, may hold values from 0.1 to 1.9
- gate_weight: bfloat16 [2048, 6144], P('blk', 'uly'), may hold values from -0.125 to 0.125
- up_weight: bfloat16 [2048, 6144], P('blk', 'uly'), may hold values from -0.125 to 0.125
- down_weight: bfloat16 [6144, 2048], P('uly', 'blk'), may hold values from -0.078125 to 0.078125
Outputs:
- layer_out: bfloat16 [6144, 2048], P(('blk', 'uly'))
Inputs may be any that keep to these rules, and one draw needn't show every extreme that they name: `positions`: each of 0 to 6143 appears once.
All inputs are finite; a program needn't handle non-finite values.
Results may differ from a plain program's by a relative error of at most 0.014.
Values may be sent and summed in bfloat16 or wider, within the bound.
A program may use at most 64 MiB of HBM per device.

v0:
```python
import math

import jax
import jax.numpy as jnp
from jax import lax
from jax.sharding import PartitionSpec as P

HEAD_SIZE = 128


def per_device(
    residual,
    query_projection,
    key_projection,
    value_projection,
    gate_proj,
    positions,
    prefix_len,
    out_weight,
    norm_gain,
    gate_weight,
    up_weight,
    down_weight,
):
    q_loc, k_loc, v_loc, g_loc = (
        lax.all_to_all(query_projection, "uly", split_axis=1, concat_axis=0, tiled=True),
        lax.all_to_all(key_projection, "uly", split_axis=1, concat_axis=0, tiled=True),
        lax.all_to_all(value_projection, "uly", split_axis=1, concat_axis=0, tiled=True),
        lax.all_to_all(gate_proj, "uly", split_axis=1, concat_axis=0, tiled=True),
    )
    row_count = q_loc.shape[0]
    kv_heads = k_loc.shape[1] // HEAD_SIZE
    q_heads = q_loc.shape[1] // HEAD_SIZE
    heads_per_group = q_heads // kv_heads
    score_scale = 1.0 / math.sqrt(HEAD_SIZE)
    blk_index = lax.axis_index("blk")
    query_pos = lax.dynamic_slice_in_dim(positions, blk_index * row_count, row_count)
    prefix = prefix_len[0]
    query_heads = q_loc.reshape(row_count, kv_heads, heads_per_group, HEAD_SIZE)
    wo_full, wg_full, wu_full, wd_full = (
        lax.all_gather(out_weight, "blk", axis=1, tiled=True),
        lax.all_gather(gate_weight, "blk", axis=0, tiled=True),
        lax.all_gather(up_weight, "blk", axis=0, tiled=True),
        lax.all_gather(down_weight, "blk", axis=1, tiled=True),
    )
    run_max = jnp.full((row_count, kv_heads, heads_per_group), -jnp.inf, jnp.float32)
    run_sum = jnp.zeros((row_count, kv_heads, heads_per_group), jnp.float32)
    weighted = jnp.zeros((row_count, kv_heads, heads_per_group, HEAD_SIZE), jnp.float32)
    key_part = lax.all_gather(k_loc, "blk", axis=0, tiled=True)
    value_part = lax.all_gather(v_loc, "blk", axis=0, tiled=True)
    key_count = key_part.shape[0]
    scores = (
        jnp.einsum(
            "bkgd,skd->bkgs",
            query_heads,
            key_part.reshape(key_count, kv_heads, HEAD_SIZE),
            preferred_element_type=jnp.float32,
        )
        * score_scale
    )
    visible = (positions[None, :] <= query_pos[:, None]) | (positions[None, :] < prefix)
    scores = jnp.where(visible[:, None, None, :], scores, -jnp.inf)
    new_max = jnp.max(scores, axis=-1)
    safe_max = jnp.where(new_max == -jnp.inf, 0.0, new_max)
    factor = jnp.exp(run_max - safe_max)
    exp_scores = jnp.exp(scores - safe_max[..., None])
    run_sum = run_sum * factor + jnp.sum(exp_scores, axis=-1)
    probs = exp_scores.astype(jnp.bfloat16)
    weighted = weighted * factor[..., None] + jnp.einsum(
        "bkgs,skd->bkgd",
        probs,
        value_part.reshape(key_count, kv_heads, HEAD_SIZE),
        preferred_element_type=jnp.float32,
    )
    _, denom, weighted = (new_max, run_sum, weighted)
    attended = (weighted / denom[..., None]).reshape(row_count, q_heads * HEAD_SIZE)
    gated_out = (attended * jax.nn.sigmoid(g_loc.astype(jnp.float32))).astype(jnp.bfloat16)
    head_partial = jnp.dot(gated_out, wo_full, preferred_element_type=jnp.float32)
    projected = lax.psum_scatter(
        head_partial.astype(jnp.bfloat16), "uly", scatter_dimension=0, tiled=True
    ).astype(jnp.float32)
    hidden_f = (residual.astype(jnp.float32) + projected).astype(jnp.bfloat16).astype(jnp.float32)
    mean_sq = jnp.mean(hidden_f * hidden_f, axis=-1, keepdims=True)
    normed = (hidden_f * lax.rsqrt(mean_sq + 1e-06) * norm_gain).astype(jnp.bfloat16)
    group_rows = lax.all_gather(normed, "uly", axis=0, tiled=True)
    gate_sum = jnp.dot(group_rows, wg_full, preferred_element_type=jnp.float32)
    up_sum = jnp.dot(group_rows, wu_full, preferred_element_type=jnp.float32)
    activated = (jax.nn.silu(gate_sum) * up_sum).astype(jnp.bfloat16)
    ffn_partial = jnp.dot(activated, wd_full, preferred_element_type=jnp.float32)
    ffn_out = lax.psum_scatter(
        ffn_partial.astype(jnp.bfloat16), "uly", scatter_dimension=0, tiled=True
    ).astype(jnp.float32)
    return (hidden_f + ffn_out).astype(jnp.bfloat16)


def solution(mesh):
    return jax.shard_map(
        per_device,
        mesh=mesh,
        in_specs=(
            P(("blk", "uly"), None),
            P(("blk", "uly"), None),
            P(("blk", "uly"), None),
            P(("blk", "uly"), None),
            P(("blk", "uly"), None),
            P(),
            P(),
            P("uly", "blk"),
            P(),
            P("blk", "uly"),
            P("blk", "uly"),
            P("uly", "blk"),
        ),
        out_specs=P(("blk", "uly"), None),
        check_vma=False,
    )
```

profile of v0, /device:TPU:1, one launch (start us, length us, event | category | flops | bytes accessed | tf_op | source)
XLA Modules:
  0.0 897.3 jit_solution(13046254227862782462)
XLA Ops:
  6.5 0.8 copy.27
  7.3 14.2 %all_to_all.67 = bf16[12,8,128]{2,0,1:T(8,128)(2,1)S(1)} all-to-all(bf16[12,8,128]{2,0,1:T(8,128)(2,1)S(1)} %copy.21), channel_id=1, replica_groups=mesh['blk'=64,'uly'=8] {'uly'}, dimensions={1} | all-to-all | bytes 49152 | tf_op jit(solution)/shard_map/all_to_all | solution.py:27
  21.5 0.6 all_to_all.53
  22.1 0.0 all-gather.8.cloned.1.call-update
  22.1 0.0 all-gather.10.cloned.1.call-start
  22.2 0.8 copy.29
  23.0 8.1 all_to_all.68
  31.1 0.6 all_to_all.60
  31.7 0.0 all-gather.10.cloned.1.call-update
  31.7 0.0 all-gather.12.cloned.1.call-start
  31.8 0.7 all-gather.12.cloned.1.call-update
  32.5 0.0 all-gather.14.cloned.1.call-start
  32.5 0.5 all-gather.14.cloned.1.call-update
  33.0 0.0 all-gather.16.cloned.1.call-start
  33.1 0.5 all-gather.16.cloned.1.call-update
  33.6 0.9 copy.28
  34.6 0.7 copy.22
  35.3 4.0 all-to-all-start.1
  39.3 0.0 all-gather.18.cloned.1.call-start
  39.3 0.6 all-gather.18.cloned.1.call-update
  40.5 0.9 copy.31
  41.5 0.7 copy.26
  42.2 0.8 dynamic_slice.3
  43.0 0.7 broadcast_compare_fusion
  43.7 1.5 all-to-all-done.1
  45.2 4.3 all-to-all-start.3
  49.6 1.2 compare_or_fusion
  50.8 4.6 all-to-all-done.3
  55.4 0.1 divide_bitcast_fusion
  55.5 97.2 %all-gather.8.cloned.1.call-done = bf16[6144,128]{1,0:T(8,128)(2,1)} async-done(((bf16[96,128]{1,0:T(8,128)(2,1)}), bf16[6144,128]{1,0:T(8,128)(2,1)}) %all-gather.8.cloned.1.call-update) | async-done | bytes 1572880 | tf_op jit(solution)/shard_map/all_gather | solution.py:49
  152.7 3.3 fusion.47
  156.0 1.4 fusion.2
  157.4 2.2 copy-done
  159.7 124.8 %all-gather.10.cloned.1.call-done = bf16[6144,128]{1,0:T(8,128)(2,1)} async-done(((bf16[96,128]{1,0:T(8,128)(2,1)}), bf16[6144,128]{1,0:T(8,128)(2,1)}) %all-gather.10.cloned.1.call-update) | async-done | bytes 1572880 | tf_op jit(solution)/shard_map/all_gather | solution.py:50
  284.4 5.6 fusion.26
  290.0 0.0 copy-start.1
  290.0 0.0 copy-start.2
  290.0 0.1 copy.25
  290.1 131.4 %all-gather.12.cloned.1.call-done = bf16[512,2048]{0,1:T(8,128)(2,1)} async-done(((bf16[512,32]{0,1:T(8,128)(2,1)}), bf16[512,2048]{0,1:T(8,128)(2,1)}) %all-gather.12.cloned.1.call-update) | async-done | bytes 2097168 | tf_op jit(solution)/shard_map/all_gather | solution.py:41
  421.6 2.3 convolution_convert_fusion
  423.9 21.0 %fusion = bf16[16,2048]{1,0:T(8,128)(2,1)S(1)} fusion(bf16[96,2048]{1,0:T(8,128)(2,1)S(1)} %convolution_convert_fusion), kind=kCustom, calls=%all-reduce-scatter | all-reduce-scatter fusion | flops 262145 | bytes 460800
  445.0 1.9 collective-permute-start
  446.9 2.2 collective-permute-start.1
  449.1 1.3 dynamic-slice.6
  451.1 0.0 collective-permute-done.1
  451.1 0.0 collective-permute-done
  451.1 0.4 concatenate
  451.5 0.2 fusion.38
  451.7 0.0 copy-done.2
  451.7 0.1 fusion.44
  451.8 15.2 %all-gather = bf16[8,12,2048]{2,1,0:T(8,128)(2,1)S(1)} all-gather(bf16[1,12,2048]{2,1,0:T(8,128)(2,1)S(1)} %fusion.44), channel_id=1, replica_groups=mesh['blk'=64,'uly'=8] {'uly'}, dimensions={0}, use_global_device_ids=true | all-gather | bytes 442368 | tf_op jit(solution)/shard_map/all_gather | solution.py:85
  467.0 0.1 reshape.132
  467.1 100.4 %all-gather.14.cloned.1.call-done = bf16[2048,768]{1,0:T(8,128)(2,1)} async-done(((bf16[32,768]{1,0:T(8,128)(2,1)}), bf16[2048,768]{1,0:T(8,128)(2,1)}) %all-gather.14.cloned.1.call-update) | async-done | bytes 3145744 | tf_op jit(solution)/shard_map/all_gather | solution.py:42
  567.5 2.5 fusion.48
  570.0 143.2 %all-gather.16.cloned.1.call-done = bf16[2048,768]{1,0:T(8,128)(2,1)} async-done(((bf16[32,768]{1,0:T(8,128)(2,1)}), bf16[2048,768]{1,0:T(8,128)(2,1)}) %all-gather.16.cloned.1.call-update) | async-done | bytes 3145744 | tf_op jit(solution)/shard_map/all_gather | solution.py:43
  713.3 145.8 %all-gather.18.cloned.1.call-done = bf16[768,2048]{0,1:T(8,128)(2,1)} async-done(((bf16[768,32]{0,1:T(8,128)(2,1)}), bf16[768,2048]{0,1:T(8,128)(2,1)}) %all-gather.18.cloned.1.call-update) | async-done | bytes 3145744 | tf_op jit(solution)/shard_map/all_gather | solution.py:44
  859.0 4.6 convolution_convert_fusion.1
  863.6 20.3 %fusion.1 = bf16[16,2048]{1,0:T(8,128)(2,1)S(1)} fusion(bf16[96,2048]{1,0:T(8,128)(2,1)S(1)} %convolution_convert_fusion.1), kind=kCustom, calls=%all-reduce-scatter.1 | all-reduce-scatter fusion | flops 262145 | bytes 460800
  883.9 1.9 collective-permute-start.2
  885.8 2.3 collective-permute-start.3
  888.1 1.3 collective-permute-done.3
  889.4 0.0 collective-permute-done.2
  889.4 0.4 concatenate.1
  889.8 0.7 fusion.41
  (16 shorter events, 0.2 us)
Async XLA Ops:
  6.5 146.1 %all-gather.8.cloned.1.call-start = ((), (), s32[]{:S(2)}) async-start(), calls=%async_computation.4 | async-start | bytes 1597440 | tf_op jit(solution)/shard_map/all_gather | solution.py:49
  22.1 262.3 %all-gather.10.cloned.1.call-start = ((), (), s32[]{:S(2)}) async-start(), calls=%async_computation.5 | async-start | bytes 1597440 | tf_op jit(solution)/shard_map/all_gather | solution.py:50
  31.7 389.9 %all-gather.12.cloned.1.call-start = ((), (), s32[]{:S(2)}) async-start(), calls=%async_computation.6 | async-start | bytes 2129920 | tf_op jit(solution)/shard_map/all_gather | solution.py:41
  32.5 535.0 %all-gather.14.cloned.1.call-start = ((), (), s32[]{:S(2)}) async-start(), calls=%async_computation.7 | async-start | bytes 3194880 | tf_op jit(solution)/shard_map/all_gather | solution.py:42
  33.0 680.2 %all-gather.16.cloned.1.call-start = ((), (), s32[]{:S(2)}) async-start(), calls=%async_computation.8 | async-start | bytes 3194880 | tf_op jit(solution)/shard_map/all_gather | solution.py:43
  35.3 10.0 %all-to-all-start.1 = ((bf16[12,8,512]{2,0,1:T(8,128)(2,1)}), bf16[12,8,512]{2,0,1:T(8,128)(2,1)S(1)}, u32[]{:S(2)}, u32[]{:S(2)}) async-start(bf16[12,8,512]{2,0,1:T(8,128)(2,1)} %copy.22), calls=%async_computation.1 | async-start | bytes 262144 | tf_op jit(solution)/shard_map/all_to_all | solution.py:26
  39.3 819.7 %all-gather.18.cloned.1.call-start = ((), (), s32[]{:S(2)}) async-start(), calls=%async_computation.9 | async-start | bytes 3194880 | tf_op jit(solution)/shard_map/all_gather | solution.py:44
  45.2 10.2 %all-to-all-start.3 = ((bf16[12,8,512]{2,0,1:T(8,128)(2,1)}), bf16[12,8,512]{2,0,1:T(8,128)(2,1)S(1)}, u32[]{:S(2)}, u32[]{:S(2)}) async-start(bf16[12,8,512]{2,0,1:T(8,128)(2,1)} %copy.26), calls=%async_computation.3 | async-start | bytes 262144 | tf_op jit(solution)/shard_map/all_to_all | solution.py:29
  156.0 3.7 copy-start
  290.0 161.5 %copy-start.1 = (bf16[12,2048]{1,0:T(8,128)(2,1)S(1)}, bf16[12,2048]{1,0:T(8,128)(2,1)}, u32[]{:S(2)}) copy-start(bf16[12,2048]{1,0:T(8,128)(2,1)} %param.12) | copy-start | bytes 147460
  290.0 161.7 %copy-start.2 = (f32[2048]{0:T(1024)S(1)}, f32[2048]{0:T(1024)}, u32[]{:S(2)}) copy-start(f32[2048]{0:T(1024)} %param.20) | copy-start | bytes 24580
  445.0 6.1 collective-permute-start
  446.9 4.1 collective-permute-start.1
  883.9 5.5 collective-permute-start.2
  885.8 3.6 collective-permute-start.3
Sparse Core Ops, SparseCore 0:
  22.3 130.3 all-gather.7
  157.1 127.2 all-gather.9
  288.9 132.6 all-gather.11
  425.9 141.5 all-gather.13
  571.8 141.4 all-gather.15
  717.6 141.4 all-gather.17
where the time goes:
time: 898 us; the launch traced here: 897 us
  waiting for transfers between devices  753 us (84%)
  blocking collectives  78.8 us (9%)
  matrix products  18.3 us (2%)
  starting transfers between devices  16.9 us (2%)
  between operations  15 us (2%)
  local copies, waits for them, and re-layouts  11.4 us (1%)
    all_gather x1, waiting for transfers between devices, per_device(): lax.all_gather(down_weight, 'blk', axis=1, tiled=True)  146 us
    all_gather x1, waiting for transfers between devices, per_device(): lax.all_gather(up_weight, 'blk', axis=0, tiled=True)  143 us
    all_gather x1, waiting for transfers between devices, per_device(): lax.all_gather(out_weight, 'blk', axis=1, tiled=True)  131 us
    all_gather x1, waiting for transfers between devices, per_device(): value_part = lax.all_gather(v_loc, 'blk', axis=0, tiled=True)  125 us
    all_gather x1, waiting for transfers between devices, per_device(): lax.all_gather(gate_weight, 'blk', axis=0, tiled=True)  100 us
    all_gather x1, waiting for transfers between devices, per_device(): key_part = lax.all_gather(k_loc, 'blk', axis=0, tiled=True)  97.2 us
    unnamed x2, blocking collectives  41.3 us
  transfers between devices with their start and end apart: 12, of which 9 were waited for; matrix products, arithmetic and copies ran while one was open for 5% of the time, Pallas kernels for 0%

commit v1 on v0

v1 whole, which is shorter than its diff:
```python
import functools
import math

import jax
import jax.numpy as jnp
from jax import lax
from jax.experimental import pallas as pl
from jax.experimental.pallas import tpu as pltpu
from jax.sharding import PartitionSpec as P

MESH = pl.DeviceIdType.MESH
HEAD_SIZE = 128
GROUP = 4
NX, NY = 4, 8
TOK = 12
PAD = 16
D = 2048
FFC = 768
CHUNK = 768
F32 = jnp.float32
BF16 = jnp.bfloat16
NEG = -1e30


def remote(src, dst, ss, rs, dest):
    return pltpu.make_async_remote_copy(
        src_ref=src, dst_ref=dst, send_sem=ss, recv_sem=rs, device_id=dest, device_id_type=MESH
    )


class Ring:
    def __init__(self, get, half, me, n, to, ss, rs):
        self.get, self.half, self.me, self.n, self.to, self.ss, self.rs = get, half, me, n, to, ss, rs
        self.sent = []

    def pos(self, d):
        return lax.rem(self.me + (d + self.n), self.n)

    def send(self, ref, way, t):
        step = 1 if way == 0 else -1
        cp = remote(ref, ref, self.ss.at[way, t], self.rs.at[way, t], self.to(self.pos(step)))
        cp.start()
        self.sent.append(cp)

    def wait(self, ref, way, t):
        remote(ref, ref, self.ss.at[way, t], self.rs.at[way, t], self.to(self.pos(1))).wait_recv()

    def start(self):
        own = self.get(self.me)
        self.send(own, 0, 0)
        self.send(own, 1, 0)

    def step(self, t):
        h = self.n // 2
        for way in (0, 1):
            j = self.pos(-t if way == 0 else t)
            self.wait(self.get(j), way, t - 1)
            self.send(self.get(j) if t < h - 1 else self.half(j, way), way, t)

    def finish(self):
        h = self.n // 2
        j = self.pos(h)
        for way in (0, 1):
            self.wait(self.half(j, way), way, h - 1)


def kernel(
    q_ref, k_ref, v_ref, g_ref, res_ref, tq_ref, posk_ref, gain_ref, wo_ref, wg_ref, wu_ref, wd_ref,
    out_ref,
    q16, k16, v16, g16, krec, vrec, qrec, grec, cmp_buf,
    bufk, bufv, bufo, bufg, bufu, bufd,
    m_sc, l_sc, acc, gated, pbuf, rbuf, hid, nrm, nbuf, act,
    a_ss, a_rs, w_ss, w_rs, x_ss, x_rs, y_ss, y_rs, c_ss, c_rs, r_ss, r_rs, n_ss, n_rs, f_ss, f_rs,
):
    blk, uly = lax.axis_index("blk"), lax.axis_index("uly")
    x, y, zh = lax.div(blk, 16), lax.rem(lax.div(blk, 2), 8), lax.rem(blk, 2)
    zl, c = lax.div(uly, 2), lax.rem(uly, 2)
    z = zh * 4 + zl

    def dev(x_, y_, zh_, zl_, c_):
        return ((x_ * NY + y_) * 2 + zh_, zl_ * 2 + c_)

    home = zh == c

    q16[0:TOK, :] = q_ref[...]
    k16[0:TOK, :] = k_ref[...]
    v16[0:TOK, :] = v_ref[...]
    g16[0:TOK, :] = g_ref[...]

    def out_peer(d):
        z2 = lax.rem(z + d, 8)
        zh2, zl2 = lax.div(z2, 4), lax.rem(z2, 4)
        return dev(x, y, zh2, zl2, zh), zl2 * 2 + zh2

    def in_peer(d):
        s = lax.rem(uly + d, 8)
        return dev(x, y, c, lax.div(s, 2), lax.rem(s, 2)), s

    other = dev(x, y, zh, zl, 1 - c)
    xto = lambda p: dev(p, y, zh, zl, c)
    yto = lambda p: dev(x, p, zh, zl, c)

    barrier = pltpu.get_barrier_semaphore()

    def greet(dest):
        pl.semaphore_signal(barrier, inc=1, device_id=dest, device_id_type=MESH)

    for d in (1, NX - 1):
        greet(xto(lax.rem(x + d, NX)))
    for d in (1, NY - 1):
        greet(yto(lax.rem(y + d, NY)))
    greet(other)
    for d in range(8):
        def both(d=d):
            greet(out_peer(d)[0])
            greet(in_peer(d)[0])
        if d == 0:
            pl.when(jnp.logical_not(home))(both)
        else:
            both()
    pl.when(home)(lambda: pl.semaphore_wait(barrier, 19))
    pl.when(jnp.logical_not(home))(lambda: pl.semaphore_wait(barrier, 21))

    order = (4, 3, 5, 2, 6, 1, 7, 0)

    def spread(src, dst, ss, rs):
        def make(d):
            dest, head = out_peer(d)
            return src(head), dst.at[uly], ss.at[d], rs.at[uly], dest
        return make

    def collect(src, dst, ss, rs):
        def make(d):
            dest, slot = in_peer(d)
            return src(slot), dst.at[zl * 2 + zh], ss.at[d], rs.at[zl * 2 + zh], dest
        return make

    def send_all(make):
        for d in order:
            s, t, a, b, dest = make(d)
            if d == 0:
                pl.when(home)(lambda s=s, t=t, b=b: pltpu.make_async_copy(s, t, b).start())
                pl.when(jnp.logical_not(home))(lambda s=s, t=t, a=a, b=b, dest=dest: remote(s, t, a, b, dest).start())
            else:
                remote(s, t, a, b, dest).start()

    def wait_all_sent(make):
        for d in order:
            s, t, a, b, dest = make(d)
            if d == 0:
                pl.when(jnp.logical_not(home))(lambda s=s, t=t, a=a, b=b, dest=dest: remote(s, t, a, b, dest).wait_send())
            else:
                remote(s, t, a, b, dest).wait_send()

    def wait_all_recv(dst, ss, rs):
        for i in range(8):
            remote(dst.at[i], dst.at[i], ss.at[i], rs.at[i], other).wait_recv()

    def cols(ref, width):
        return lambda head: ref.at[:, pl.ds(pl.multiple_of(head * width, 128), width)]

    moves = [
        spread(cols(k16, HEAD_SIZE), krec, a_ss.at[0], a_rs.at[0]),
        spread(cols(v16, HEAD_SIZE), vrec, a_ss.at[1], a_rs.at[1]),
        spread(cols(q16, GROUP * HEAD_SIZE), qrec, a_ss.at[2], a_rs.at[2]),
        spread(cols(g16, GROUP * HEAD_SIZE), grec, a_ss.at[3], a_rs.at[3]),
    ]
    send_all(moves[0])
    send_all(moves[1])

    weights = [(wo_ref, bufo), (wg_ref, bufg), (wu_ref, bufu), (wd_ref, bufd)]
    twin = dev(x, y, c, zl, zh)

    def swap(i):
        src, buf = weights[i]
        return src, buf.at[x, y, zh], w_ss.at[i], w_rs.at[i], twin

    def swap_start():
        for i in range(4):
            s, t, a, b, dest = swap(i)
            pl.when(home)(lambda s=s, t=t, b=b: pltpu.make_async_copy(s, t, b).start())
            pl.when(jnp.logical_not(home))(lambda s=s, t=t, a=a, b=b, dest=dest: remote(s, t, a, b, dest).start())

    def swap_wait(i):
        own = weights[i][1].at[x, y, c]
        remote(own, own, w_ss.at[i], w_rs.at[i], other).wait_recv()

    swap_start()
    send_all(moves[2])
    send_all(moves[3])

    sent = []

    def gather(buf, idx, x_first, rows):
        rx = dict(n=NX, me=x, to=xto, ss=x_ss.at[idx], rs=x_rs.at[idx])
        ry = dict(n=NY, me=y, to=yto, ss=y_ss.at[idx], rs=y_rs.at[idx])
        hr = rows // 2
        if x_first:
            one = Ring(lambda i: buf.at[i, y, c], lambda i, w: buf.at[i, y, c, pl.ds(w * hr, hr)], **rx)
            two = Ring(lambda i: buf.at[:, i, c], lambda i, w: buf.at[pl.ds(w * 2, 2), i, c], **ry)
            theirs = lambda i: buf.at[:, i, 1 - c]
        else:
            one = Ring(lambda i: buf.at[x, i, c], lambda i, w: buf.at[x, i, c, pl.ds(w * hr, hr)], **ry)
            two = Ring(lambda i: buf.at[i, :, c], lambda i, w: buf.at[i, pl.ds(w * 4, 4), c], **rx)
            theirs = lambda i: buf.at[i, :, 1 - c]

        def give(j, t):
            cp = remote(two.get(j), two.get(j), c_ss.at[idx, t], c_rs.at[idx, t], other)
            cp.start()
            sent.append(cp)

        one.start()
        yield
        for t in range(1, one.n // 2):
            one.step(t)
            yield
        one.finish()
        yield
        two.start()
        give(two.me, 0)
        yield
        for t in range(1, two.n // 2):
            two.step(t)
            give(two.pos(-t), 2 * t - 1)
            give(two.pos(t), 2 * t)
            yield
        two.finish()
        give(two.pos(two.n // 2), two.n - 1)
        yield
        for t in range(two.n):
            d = 0 if t == 0 else (-(t + 1) // 2 if t % 2 else t // 2)
            if t == two.n - 1:
                d = two.n // 2
            ref = theirs(two.pos(d))
            remote(ref, ref, c_ss.at[idx, t], c_rs.at[idx, t], other).wait_recv()
        sent.extend(one.sent + two.sent)
        yield

    def compact(rec, buf):
        for s in range(8):
            cmp_buf[TOK * s:TOK * (s + 1), :] = rec[s].astype(F32)[:TOK]
        buf[x, y, c] = cmp_buf[...].astype(BF16)

    gk = gather(bufk, 0, True, 96)
    gv = gather(bufv, 1, False, 96)
    go = gather(bufo, 2, True, 32)
    gg = gather(bufg, 3, True, 32)
    gu = gather(bufu, 4, False, 32)
    gd = gather(bufd, 5, False, 32)

    def run(gens, times):
        for _ in range(times):
            for gen in gens:
                next(gen, None)

    wait_all_recv(krec, a_ss.at[0], a_rs.at[0])
    compact(krec, bufk)
    next(gk)
    wait_all_recv(vrec, a_ss.at[1], a_rs.at[1])
    compact(vrec, bufv)
    next(gv)
    for i in range(4):
        swap_wait(i)
    run([gk, gv, go, gg, gu, gd], 2)
    run([gk, gv], 2)
    run([gk, gv, go, gg, gu, gd], 1)
    run([gk, gv], 2)
    run([gu, gd], 2)
    run([go, gg, gu, gd], 1)
    run([gk, gv], 9)
    wait_all_recv(qrec, a_ss.at[2], a_rs.at[2])
    wait_all_recv(grec, a_ss.at[3], a_rs.at[3])

    m_sc[...] = jnp.full_like(m_sc, NEG)
    l_sc[...] = jnp.zeros_like(l_sc)
    acc[...] = jnp.zeros_like(acc)
    scale = 1.0 / math.sqrt(HEAD_SIZE)

    def attend(i, _):
        xi, yi = lax.div(i, 2), lax.rem(i, 2) * 4
        keys = bufk[xi, pl.ds(yi, 4)].reshape(CHUNK, HEAD_SIZE)
        vals = bufv[xi, pl.ds(yi, 4)].reshape(CHUNK, HEAD_SIZE)
        visible = posk_ref[i] <= tq_ref[...]
        for g in range(GROUP):
            q = qrec[:, :, g * HEAD_SIZE:(g + 1) * HEAD_SIZE].reshape(8 * PAD, HEAD_SIZE)
            s = lax.dot_general(q, keys, (((1,), (1,)), ((), ())), preferred_element_type=F32) * scale
            s = jnp.where(visible, s, NEG)
            old = m_sc[g]
            new = jnp.maximum(old, jnp.max(s, axis=1, keepdims=True))
            p = jnp.exp(s - new)
            f = jnp.exp(old - new)
            l_sc[g] = l_sc[g] * f + jnp.sum(p, axis=1, keepdims=True)
            acc[g] = acc[g] * f + jnp.dot(p.astype(BF16), vals, preferred_element_type=F32)
            m_sc[g] = new
        return 0

    lax.fori_loop(0, 8, attend, 0)
    for g in range(GROUP):
        gate = grec[:, :, g * HEAD_SIZE:(g + 1) * HEAD_SIZE].reshape(8 * PAD, HEAD_SIZE).astype(F32)
        gated[:, g * HEAD_SIZE:(g + 1) * HEAD_SIZE] = (acc[g] / l_sc[g] * jax.nn.sigmoid(gate)).astype(BF16)

    run([go, gg, gu, gd], 9)

    NT = (((1,), (1,)), ((), ()))

    def project(lhs, buf, width):
        def body(i, _):
            w = buf[i].reshape(512, width)
            part = lax.dot_general(lhs, w, NT, preferred_element_type=F32).astype(BF16)
            pbuf[:, :, pl.ds(pl.multiple_of(i * 512, 128), 512)] = part.reshape(8, PAD, 512)
            return 0
        lax.fori_loop(0, NX, body, 0)

    block = lambda s: pbuf.at[s]

    def total():
        t = rbuf[0].astype(F32)
        for i in range(1, 8):
            t = t + rbuf[i].astype(F32)
        return t

    project(gated[...], bufo, 512)
    first = collect(block, rbuf, r_ss, r_rs)
    send_all(first)
    wait_all_recv(rbuf, r_ss, r_rs)
    hid[0:TOK, :] = (res_ref[...].astype(F32) + total()[:TOK]).astype(BF16)
    hf = hid[...].astype(F32)
    mean_sq = jnp.mean(hf * hf, axis=-1, keepdims=True)
    nrm[...] = (hf * lax.rsqrt(mean_sq + 1e-06) * gain_ref[...]).astype(BF16)
    normed = spread(lambda head: nrm, nbuf, n_ss, n_rs)
    send_all(normed)
    wait_all_recv(nbuf, n_ss, n_rs)

    rows = nbuf[...].reshape(8 * PAD, D)
    for n in range(FFC // 256):
        at = slice(n * 256, (n + 1) * 256)
        gate_sum = jnp.zeros((8 * PAD, 256), F32)
        up_sum = jnp.zeros((8 * PAD, 256), F32)
        for i in range(NX):
            r = rows[:, i * 512:(i + 1) * 512]
            gate_sum += jnp.dot(r, bufg[i, :, :, :, at].reshape(512, 256), preferred_element_type=F32)
            up_sum += jnp.dot(r, bufu[i, :, :, :, at].reshape(512, 256), preferred_element_type=F32)
        act[:, at] = (jax.nn.silu(gate_sum) * up_sum).astype(BF16)

    wait_all_sent(first)
    project(act[...], bufd, FFC)
    last = collect(block, rbuf, f_ss, f_rs)
    send_all(last)
    wait_all_recv(rbuf, f_ss, f_rs)
    out_ref[...] = (hid[...].astype(F32) + total())[:TOK].astype(BF16)

    wait_all_sent(last)
    wait_all_sent(normed)
    for m in moves:
        wait_all_sent(m)
    for i in range(4):
        s, t, a, b, dest = swap(i)
        pl.when(jnp.logical_not(home))(lambda s=s, t=t, a=a, b=b, dest=dest: remote(s, t, a, b, dest).wait_send())
    for cp in sent:
        cp.wait_send()


def per_device(
    residual, query_projection, key_projection, value_projection, gate_proj, positions, prefix_len,
    out_weight, norm_gain, gate_weight, up_weight, down_weight,
):
    blk, uly = lax.axis_index("blk"), lax.axis_index("uly")
    first = (blk // 2 * 2 + uly % 2) * 96
    mine = lax.dynamic_slice_in_dim(positions, first, 96).reshape(8, TOK)
    tq = jnp.maximum(jnp.pad(mine, ((0, 0), (0, PAD - TOK))), prefix_len[0] - 1).reshape(8 * PAD, 1)
    posk = positions.reshape(8, 1, CHUNK)
    vm = pl.BlockSpec(memory_space=pltpu.VMEM)
    dma = pltpu.SemaphoreType.DMA
    half = lambda r, w: pltpu.VMEM((NX, NY, 2, r, w), BF16)
    return pl.pallas_call(
        kernel,
        out_shape=jax.ShapeDtypeStruct((TOK, D), BF16),
        in_specs=[vm] * 12,
        out_specs=vm,
        scratch_shapes=[
            pltpu.VMEM((PAD, 4096), BF16),
            pltpu.VMEM((PAD, 1024), BF16),
            pltpu.VMEM((PAD, 1024), BF16),
            pltpu.VMEM((PAD, 4096), BF16),
            pltpu.VMEM((8, PAD, 128), BF16),
            pltpu.VMEM((8, PAD, 128), BF16),
            pltpu.VMEM((8, PAD, 512), BF16),
            pltpu.VMEM((8, PAD, 512), BF16),
            pltpu.VMEM((96, 128), F32),
            half(96, 128), half(96, 128), half(32, 512), half(32, FFC), half(32, FFC), half(32, FFC),
            pltpu.VMEM((GROUP, 8 * PAD, 1), F32),
            pltpu.VMEM((GROUP, 8 * PAD, 1), F32),
            pltpu.VMEM((GROUP, 8 * PAD, HEAD_SIZE), F32),
            pltpu.VMEM((8 * PAD, GROUP * HEAD_SIZE), BF16),
            pltpu.VMEM((8, PAD, D), BF16),
            pltpu.VMEM((8, PAD, D), BF16),
            pltpu.VMEM((PAD, D), BF16),
            pltpu.VMEM((PAD, D), BF16),
            pltpu.VMEM((8, PAD, D), BF16),
            pltpu.VMEM((8 * PAD, FFC), BF16),
            dma((4, 8)), dma((4, 8)),
            dma((4,)), dma((4,)),
            dma((6, 2, 2)), dma((6, 2, 2)),
            dma((6, 2, 4)), dma((6, 2, 4)),
            dma((6, 8)), dma((6, 8)),
            dma((8,)), dma((8,)),
            dma((8,)), dma((8,)),
            dma((8,)), dma((8,)),
        ],
        compiler_params=pltpu.CompilerParams(
            collective_id=0, has_side_effects=True, vmem_limit_bytes=60 * 2**20
        ),
        name="layer",
    )(
        query_projection, key_projection, value_projection, gate_proj, residual, tq, posk,
        norm_gain.reshape(1, D), out_weight.T, gate_weight, up_weight, down_weight.T,
    )


def solution(mesh):
    return jax.shard_map(
        per_device,
        mesh=mesh,
        in_specs=(
            P(("blk", "uly"), None),
            P(("blk", "uly"), None),
            P(("blk", "uly"), None),
            P(("blk", "uly"), None),
            P(("blk", "uly"), None),
            P(),
            P(),
            P("uly", "blk"),
            P(),
            P("blk", "uly"),
            P("blk", "uly"),
            P("uly", "blk"),
        ),
        out_specs=P(("blk", "uly"), None),
        check_vma=False,
    )
```

time: 898 us -> 142 us (0.16)
  waiting for transfers between devices: 753 us -> 0 us
  Pallas kernels: 0 us -> 138 us
  blocking collectives: 78.8 us -> 0 us
  matrix products: 18.3 us -> 0 us
  starting transfers between devices: 16.9 us -> 0 us
  between operations: 15 us -> 0.66 us
    all_gather x6 -> x0, waiting for transfers between devices: 743 us -> none  [the longest x1 146 us: per_device(): lax.all_gather(down_weight, 'blk', axis=1, tiled=True)]
    pallas_call x0 -> x1, Pallas kernels: none -> 138 us  [per_device(): pl.pallas_call(kernel, out_shape=jax.ShapeDtypeStruct((TOK, D), BF16), in...]
    unnamed x2 -> x0, blocking collectives: 41.3 us -> none
    all_to_all x2 -> x0, blocking collectives: 22.3 us -> none  [the longest x1 14.2 us: per_device(): lax.all_to_all(key_projection, 'uly', split_axis=1, concat_axis=0, tiled=...]
    dot_general x5 -> x0, matrix products: 18.3 us -> none  [the longest x1 5.57 us: per_device(): jnp.einsum('bkgs,skd->bkgd', probs, value_part.reshape(key_count, kv_head...]
    all_gather x1 -> x0, blocking collectives: 15.2 us -> none  [per_device(): group_rows = lax.all_gather(normed, 'uly', axis=0, tiled=True)]
  transfers between devices with their start and end apart: 12 -> 0, of which waited for: 9 -> 0; matrix products, arithmetic and copies ran while one was open for 5% -> 0% of each run, Pallas kernels for 0% -> 0%
where the time goes in v1:
time: 142 us
  Pallas kernels  138 us (97%)
  local copies, waits for them, and re-layouts  3.05 us (2%)
    pallas_call x1, Pallas kernels, per_device(): pl.pallas_call(kernel, out_shape=jax.ShapeDtypeStruct((TOK, D), BF16), in...  138 us

profile of v1, /device:TPU:1, one launch (start us, length us, event | category | flops | bytes accessed | tf_op | source)
XLA Modules:
  0.0 142.1 jit_solution(7583662409644583058)
XLA Ops:
  0.7 0.8 dynamic_slice.3
  1.4 0.1 reshape.14
  1.5 0.7 reshape.18.tq_ref
  2.2 138.4 %layer.1 = bf16[12,2048]{1,0:T(8,128)(2,1)} custom-call(bf16[12,4096]{1,0:T(8,128)(2,1)} %q_ref.1, bf16[12,1024]{1,0:T(8,128)(2,1)} %k_ref.1, bf16[12,1024]{1,0:T(8,128)(2,1)} %v_ref.1, bf16[12,4096]{1,0:T(8,128)(2,1)} %g_ref.1, bf16[12,2048]{1,0:T(8,128)(2,1)} %res_ref.1, s32[128,1]{1,0:T(8,128)} %reshape.18.tq_ref, s32[8,1,768]{2,1,0:T(1,128)} %bitcast.7, ...), custom_call_target="tpu_custom_call" | custom-call | tf_op jit(solution)/shard_map/layer/pallas_call | solution.py:375
  140.7 1.5 %copy.16 = bf16[12,2048]{1,0:T(8,128)(2,1)} copy(bf16[12,2048]{1,0:T(8,128)(2,1)} %layer.1) | data formatting | bytes 98304
  (1 shorter events, 0.0 us)

commit v2 on v1

--- a/solution.py
+++ b/solution.py
@@ -20,6 +20,7 @@
 F32 = jnp.float32
 BF16 = jnp.bfloat16
 NEG = -1e30
+STAGE = 99
 
 
 def remote(src, dst, ss, rs, dest):
@@ -29,9 +30,9 @@
 
 
 class Ring:
-    def __init__(self, get, half, me, n, to, ss, rs):
+    def __init__(self, get, half, me, n, to, ss, rs, log):
         self.get, self.half, self.me, self.n, self.to, self.ss, self.rs = get, half, me, n, to, ss, rs
-        self.sent = []
+        self.sent = log
 
     def pos(self, d):
         return lax.rem(self.me + (d + self.n), self.n)
@@ -64,12 +65,49 @@
             self.wait(self.half(j, way), way, h - 1)
 
 
+class Direct:
+    def __init__(self, get, me, n, to, ss, rs, log):
+        self.get, self.me, self.n, self.to, self.ss, self.rs, self.sent = get, me, n, to, ss, rs, log
+
+    def pos(self, d):
+        return lax.rem(self.me + d, self.n)
+
+    def start(self):
+        own = self.get(self.me)
+        for d in range(1, self.n):
+            cp = remote(own, own, self.ss.at[d // 2, d % 2], self.rs.at[d // 2, d % 2], self.to(self.pos(d)))
+            cp.start()
+            self.sent.append(cp)
+
+    def finish(self):
+        for d in range(1, self.n):
+            ref = self.get(self.pos(self.n - d))
+            remote(ref, ref, self.ss.at[d // 2, d % 2], self.rs.at[d // 2, d % 2], self.to(self.pos(1))).wait_recv()
+
+
+def pack(v):
+    lo, hi = v[:, :8], v[:, 8:]
+    turn = lambda t: jnp.concatenate([t[:, 4:], t[:, :4]], axis=1)
+    extra = jnp.concatenate([turn(lo[..., 384:]), lo[..., 384:], turn(hi[..., 384:])], axis=2)
+    row = lax.broadcasted_iota(jnp.int32, extra.shape, 1)
+    return jnp.concatenate([lo[..., :384], jnp.where(row < 4, hi[..., :384], extra)], axis=1)
+
+
+def unpack(v):
+    lo, hi = v[:, :8], v[:, 8:]
+    turn = lambda t: jnp.concatenate([t[:, 4:], t[:, :4]], axis=1)
+    a, b, d = hi[..., :128], hi[..., 128:256], hi[..., 256:]
+    row = lax.broadcasted_iota(jnp.int32, a.shape, 1)
+    last = jnp.concatenate([jnp.where(row < 4, turn(a), b), turn(d)], axis=1)
+    return jnp.concatenate([v, last], axis=2)
+
+
 def kernel(
     q_ref, k_ref, v_ref, g_ref, res_ref, tq_ref, posk_ref, gain_ref, wo_ref, wg_ref, wu_ref, wd_ref,
     out_ref,
     q16, k16, v16, g16, krec, vrec, qrec, grec, cmp_buf,
     bufk, bufv, bufo, bufg, bufu, bufd,
-    m_sc, l_sc, acc, gated, pbuf, rbuf, hid, nrm, nbuf, act,
+    m_sc, l_sc, acc, gated, pbuf, rbuf, sbuf, fbuf, hid, nrm, nbuf, rows, act,
     a_ss, a_rs, w_ss, w_rs, x_ss, x_rs, y_ss, y_rs, c_ss, c_rs, r_ss, r_rs, n_ss, n_rs, f_ss, f_rs,
 ):
     blk, uly = lax.axis_index("blk"), lax.axis_index("uly")
@@ -86,6 +124,7 @@
     k16[0:TOK, :] = k_ref[...]
     v16[0:TOK, :] = v_ref[...]
     g16[0:TOK, :] = g_ref[...]
+    hid[0:TOK, :] = res_ref[...]
 
     def out_peer(d):
         z2 = lax.rem(z + d, 8)
@@ -105,7 +144,7 @@
     def greet(dest):
         pl.semaphore_signal(barrier, inc=1, device_id=dest, device_id_type=MESH)
 
-    for d in (1, NX - 1):
+    for d in range(1, NX):
         greet(xto(lax.rem(x + d, NX)))
     for d in (1, NY - 1):
         greet(yto(lax.rem(y + d, NY)))
@@ -118,21 +157,18 @@
             pl.when(jnp.logical_not(home))(both)
         else:
             both()
-    pl.when(home)(lambda: pl.semaphore_wait(barrier, 19))
-    pl.when(jnp.logical_not(home))(lambda: pl.semaphore_wait(barrier, 21))
-
+    pl.when(home)(lambda: pl.semaphore_wait(barrier, 20))
+    pl.when(jnp.logical_not(home))(lambda: pl.semaphore_wait(barrier, 22))
+
+    if STAGE <= 1:
+        out_ref[...] = res_ref[...]
+        return
     order = (4, 3, 5, 2, 6, 1, 7, 0)
 
     def spread(src, dst, ss, rs):
         def make(d):
             dest, head = out_peer(d)
             return src(head), dst.at[uly], ss.at[d], rs.at[uly], dest
-        return make
-
-    def collect(src, dst, ss, rs):
-        def make(d):
-            dest, slot = in_peer(d)
-            return src(slot), dst.at[zl * 2 + zh], ss.at[d], rs.at[zl * 2 + zh], dest
         return make
 
     def send_all(make):
@@ -189,20 +225,27 @@
     send_all(moves[2])
     send_all(moves[3])
 
+    def close(*makes):
+        for m in moves + list(makes):
+            wait_all_sent(m)
+        for i in range(4):
+            s, t, a, b, dest = swap(i)
+            pl.when(jnp.logical_not(home))(lambda s=s, t=t, a=a, b=b, dest=dest: remote(s, t, a, b, dest).wait_send())
+        for cp in sent:
+            cp.wait_send()
+
     sent = []
 
-    def gather(buf, idx, x_first, rows):
-        rx = dict(n=NX, me=x, to=xto, ss=x_ss.at[idx], rs=x_rs.at[idx])
-        ry = dict(n=NY, me=y, to=yto, ss=y_ss.at[idx], rs=y_rs.at[idx])
+    def gather(buf, idx, x_first, rows, theirs_too=True):
+        rx = dict(n=NX, me=x, to=xto, ss=x_ss.at[idx], rs=x_rs.at[idx], log=sent)
+        ry = dict(n=NY, me=y, to=yto, ss=y_ss.at[idx], rs=y_rs.at[idx], log=sent)
         hr = rows // 2
         if x_first:
-            one = Ring(lambda i: buf.at[i, y, c], lambda i, w: buf.at[i, y, c, pl.ds(w * hr, hr)], **rx)
+            one = Direct(lambda i: buf.at[i, y, c], **rx)
             two = Ring(lambda i: buf.at[:, i, c], lambda i, w: buf.at[pl.ds(w * 2, 2), i, c], **ry)
-            theirs = lambda i: buf.at[:, i, 1 - c]
         else:
             one = Ring(lambda i: buf.at[x, i, c], lambda i, w: buf.at[x, i, c, pl.ds(w * hr, hr)], **ry)
             two = Ring(lambda i: buf.at[i, :, c], lambda i, w: buf.at[i, pl.ds(w * 4, 4), c], **rx)
-            theirs = lambda i: buf.at[i, :, 1 - c]
 
         def give(j, t):
             cp = remote(two.get(j), two.get(j), c_ss.at[idx, t], c_rs.at[idx, t], other)
@@ -211,11 +254,11 @@
 
         one.start()
         yield
-        for t in range(1, one.n // 2):
-            one.step(t)
-            yield
+        if not x_first:
+            for t in range(1, one.n // 2):
+                one.step(t)
+                yield
         one.finish()
-        yield
         two.start()
         give(two.me, 0)
         yield
@@ -227,111 +270,178 @@
         two.finish()
         give(two.pos(two.n // 2), two.n - 1)
         yield
-        for t in range(two.n):
-            d = 0 if t == 0 else (-(t + 1) // 2 if t % 2 else t // 2)
-            if t == two.n - 1:
-                d = two.n // 2
-            ref = theirs(two.pos(d))
-            remote(ref, ref, c_ss.at[idx, t], c_rs.at[idx, t], other).wait_recv()
-        sent.extend(one.sent + two.sent)
+        if theirs_too:
+            for t in range(two.n):
+                theirs(buf, idx, x_first, t)
         yield
+
+    def place(n, t):
+        if t == n - 1:
+            return n // 2
+        return -((t + 1) // 2) if t % 2 else t // 2
+
+    def theirs(buf, idx, x_first, t):
+        if x_first:
+            ref = buf.at[:, lax.rem(y + NY + place(NY, t), NY), 1 - c]
+        else:
+            ref = buf.at[lax.rem(x + NX + place(NX, t), NX), :, 1 - c]
+        remote(ref, ref, c_ss.at[idx, t], c_rs.at[idx, t], other).wait_recv()
 
     def compact(rec, buf):
         for s in range(8):
             cmp_buf[TOK * s:TOK * (s + 1), :] = rec[s].astype(F32)[:TOK]
         buf[x, y, c] = cmp_buf[...].astype(BF16)
 
-    gk = gather(bufk, 0, True, 96)
-    gv = gather(bufv, 1, False, 96)
-    go = gather(bufo, 2, True, 32)
-    gg = gather(bufg, 3, True, 32)
-    gu = gather(bufu, 4, False, 32)
+    gk = gather(bufk, 0, True, 96, False)
+    gv = gather(bufv, 1, True, 96, False)
+    go = gather(bufo, 2, False, 32)
+    gg = gather(bufg, 3, False, 32)
+    gu = gather(bufu, 4, True, 32)
     gd = gather(bufd, 5, False, 32)
 
-    def run(gens, times):
-        for _ in range(times):
-            for gen in gens:
-                next(gen, None)
+    def go_on(*gens):
+        for gen in gens:
+            next(gen, None)
+
+    scale = 1.0 / math.sqrt(HEAD_SIZE)
+
+    def attend(first, last):
+        for t in range(first, last):
+            theirs(bufk, 0, True, t)
+            theirs(bufv, 1, True, t)
+
+        def body(i, _):
+            far = lax.div(i + 1, 2)
+            j = lax.rem(y + NY + jnp.where(jnp.logical_and(lax.rem(i, 2) == 1, i < NY - 1), -far, far), NY)
+            keys = bufk[:, j].reshape(CHUNK, HEAD_SIZE)
+            vals = bufv[:, j].reshape(CHUNK, HEAD_SIZE)
+            visible = posk_ref[j] <= tq_ref[...]
+            for g in range(GROUP):
+                q = qrec[:, :, g * HEAD_SIZE:(g + 1) * HEAD_SIZE].reshape(8 * PAD, HEAD_SIZE)
+                s = lax.dot_general(q, keys, (((1,), (1,)), ((), ())), preferred_element_type=F32) * scale
+                s = jnp.where(visible, s, NEG)
+                old = m_sc[g]
+                new = jnp.maximum(old, jnp.max(s, axis=1, keepdims=True))
+                p = jnp.exp(s - new)
+                f = jnp.exp(old - new)
+                l_sc[g] = l_sc[g] * f + jnp.sum(p, axis=1, keepdims=True)
+                acc[g] = acc[g] * f + jnp.dot(p.astype(BF16), vals, preferred_element_type=F32)
+                m_sc[g] = new
+            return 0
+
+        lax.fori_loop(first, last, body, 0)
 
     wait_all_recv(krec, a_ss.at[0], a_rs.at[0])
     compact(krec, bufk)
-    next(gk)
+    go_on(gk)
     wait_all_recv(vrec, a_ss.at[1], a_rs.at[1])
     compact(vrec, bufv)
-    next(gv)
-    for i in range(4):
-        swap_wait(i)
-    run([gk, gv, go, gg, gu, gd], 2)
-    run([gk, gv], 2)
-    run([gk, gv, go, gg, gu, gd], 1)
-    run([gk, gv], 2)
-    run([gu, gd], 2)
-    run([go, gg, gu, gd], 1)
-    run([gk, gv], 9)
-    wait_all_recv(qrec, a_ss.at[2], a_rs.at[2])
-    wait_all_recv(grec, a_ss.at[3], a_rs.at[3])
-
+    go_on(gv)
     m_sc[...] = jnp.full_like(m_sc, NEG)
     l_sc[...] = jnp.zeros_like(l_sc)
     acc[...] = jnp.zeros_like(acc)
-    scale = 1.0 / math.sqrt(HEAD_SIZE)
-
-    def attend(i, _):
-        xi, yi = lax.div(i, 2), lax.rem(i, 2) * 4
-        keys = bufk[xi, pl.ds(yi, 4)].reshape(CHUNK, HEAD_SIZE)
-        vals = bufv[xi, pl.ds(yi, 4)].reshape(CHUNK, HEAD_SIZE)
-        visible = posk_ref[i] <= tq_ref[...]
-        for g in range(GROUP):
-            q = qrec[:, :, g * HEAD_SIZE:(g + 1) * HEAD_SIZE].reshape(8 * PAD, HEAD_SIZE)
-            s = lax.dot_general(q, keys, (((1,), (1,)), ((), ())), preferred_element_type=F32) * scale
-            s = jnp.where(visible, s, NEG)
-            old = m_sc[g]
-            new = jnp.maximum(old, jnp.max(s, axis=1, keepdims=True))
-            p = jnp.exp(s - new)
-            f = jnp.exp(old - new)
-            l_sc[g] = l_sc[g] * f + jnp.sum(p, axis=1, keepdims=True)
-            acc[g] = acc[g] * f + jnp.dot(p.astype(BF16), vals, preferred_element_type=F32)
-            m_sc[g] = new
-        return 0
-
-    lax.fori_loop(0, 8, attend, 0)
+    swap_wait(0)
+    go_on(go)
+    go_on(gk, gv)
+    go_on(go)
+    for i in range(1, 4):
+        swap_wait(i)
+    go_on(gu)
+    go_on(gk, gv)
+    go_on(go)
+    wait_all_recv(qrec, a_ss.at[2], a_rs.at[2])
+    wait_all_recv(grec, a_ss.at[3], a_rs.at[3])
+    attend(0, 1)
+    go_on(gk, gv)
+    go_on(go)
+    go_on(gg)
+    attend(1, 3)
+    go_on(go)
+    go_on(gk, gv)
+    go_on(gd)
+    go_on(gg)
+    go_on(gu)
+    attend(3, 5)
+    go_on(gg, gd)
+    go_on(go)
+    go_on(gk, gv)
+    attend(5, 7)
+    go_on(gg, gd)
+    go_on(go)
+    attend(7, 8)
     for g in range(GROUP):
         gate = grec[:, :, g * HEAD_SIZE:(g + 1) * HEAD_SIZE].reshape(8 * PAD, HEAD_SIZE).astype(F32)
         gated[:, g * HEAD_SIZE:(g + 1) * HEAD_SIZE] = (acc[g] / l_sc[g] * jax.nn.sigmoid(gate)).astype(BF16)
-
-    run([go, gg, gu, gd], 9)
+    go_on(gg, gd)
+    go_on(go)
+    if STAGE <= 4:
+        go_on(*[gg, gd, gu] * 9)
+        out_ref[...] = res_ref[...]
+        close()
+        return
 
     NT = (((1,), (1,)), ((), ()))
 
-    def project(lhs, buf, width):
-        def body(i, _):
-            w = buf[i].reshape(512, width)
-            part = lax.dot_general(lhs, w, NT, preferred_element_type=F32).astype(BF16)
-            pbuf[:, :, pl.ds(pl.multiple_of(i * 512, 128), 512)] = part.reshape(8, PAD, 512)
-            return 0
-        lax.fori_loop(0, NX, body, 0)
-
-    block = lambda s: pbuf.at[s]
-
-    def total():
-        t = rbuf[0].astype(F32)
-        for i in range(1, 8):
-            t = t + rbuf[i].astype(F32)
-        return t
-
-    project(gated[...], bufo, 512)
-    first = collect(block, rbuf, r_ss, r_rs)
-    send_all(first)
-    wait_all_recv(rbuf, r_ss, r_rs)
-    hid[0:TOK, :] = (res_ref[...].astype(F32) + total()[:TOK]).astype(BF16)
-    hf = hid[...].astype(F32)
-    mean_sq = jnp.mean(hf * hf, axis=-1, keepdims=True)
-    nrm[...] = (hf * lax.rsqrt(mean_sq + 1e-06) * gain_ref[...]).astype(BF16)
+    def collect(i, out, into, ss, rs):
+        at = pl.ds(i * 384, 384)
+
+        def make(d):
+            dest, slot = in_peer(d)
+            u = zl * 2 + zh
+            return out.at[slot, :, at], into.at[u, :, at], ss.at[i, d], rs.at[i, u], dest
+        return make
+
+    def project(lhs, buf, width, out, into, ss, rs):
+        makes = []
+        for i in range(NX):
+            part = lax.dot_general(lhs, buf[i].reshape(512, width), NT, preferred_element_type=F32)
+            out[:, :, i * 384:(i + 1) * 384] = pack(part.reshape(8, PAD, 512)).astype(BF16)
+            makes.append(collect(i, out, into, ss, rs))
+            send_all(makes[-1])
+        return makes
+
+    def total(i, into, ss, rs):
+        at = slice(i * 384, (i + 1) * 384)
+        for u in range(8):
+            ref = into.at[u, :, pl.ds(i * 384, 384)]
+            remote(ref, ref, ss.at[i, u], rs.at[i, u], other).wait_recv()
+        t = into[0, :, at].astype(F32)
+        for u in range(1, 8):
+            t = t + into[u, :, at].astype(F32)
+        return unpack(t[None])[0]
+
+    parts = project(gated[...], bufo, 512, pbuf, rbuf, r_ss, r_rs)
+    go_on(gu)
+    go_on(gd)
+    square = jnp.zeros((PAD, 1), F32)
+    for i in range(NX):
+        at = slice(i * 512, (i + 1) * 512)
+        h = (hid[:, at].astype(F32) + total(i, rbuf, r_ss, r_rs)).astype(BF16)
+        hid[:, at] = h
+        h = h.astype(F32)
+        square += jnp.sum(h * h, axis=-1, keepdims=True)
+    inv = lax.rsqrt(square * (1.0 / D) + 1e-06)
+    for i in range(NX):
+        at = slice(i * 512, (i + 1) * 512)
+        nrm[:, i * 384:(i + 1) * 384] = pack((hid[:, at].astype(F32) * inv * gain_ref[:, at])[None])[0].astype(BF16)
     normed = spread(lambda head: nrm, nbuf, n_ss, n_rs)
     send_all(normed)
+    go_on(gu)
+    go_on(gg)
+    go_on(gu)
+    go_on(gd)
+    go_on(gg)
     wait_all_recv(nbuf, n_ss, n_rs)
-
-    rows = nbuf[...].reshape(8 * PAD, D)
+    for i in range(NX):
+        at = slice(i * 512, (i + 1) * 512)
+        rows[:, at] = unpack(nbuf[:, :, i * 384:(i + 1) * 384].astype(F32)).reshape(8 * PAD, 512).astype(BF16)
+    if STAGE <= 7:
+        go_on(*[gg, gd, gu] * 9)
+        out_ref[...] = res_ref[...]
+        close(normed, *parts)
+        return
+    go_on(gu)
+    go_on(gg, gu)
     for n in range(FFC // 256):
         at = slice(n * 256, (n + 1) * 256)
         gate_sum = jnp.zeros((8 * PAD, 256), F32)
@@ -341,23 +451,16 @@
             gate_sum += jnp.dot(r, bufg[i, :, :, :, at].reshape(512, 256), preferred_element_type=F32)
             up_sum += jnp.dot(r, bufu[i, :, :, :, at].reshape(512, 256), preferred_element_type=F32)
         act[:, at] = (jax.nn.silu(gate_sum) * up_sum).astype(BF16)
-
-    wait_all_sent(first)
-    project(act[...], bufd, FFC)
-    last = collect(block, rbuf, f_ss, f_rs)
-    send_all(last)
-    wait_all_recv(rbuf, f_ss, f_rs)
-    out_ref[...] = (hid[...].astype(F32) + total())[:TOK].astype(BF16)
-
-    wait_all_sent(last)
-    wait_all_sent(normed)
-    for m in moves:
-        wait_all_sent(m)
-    for i in range(4):
-        s, t, a, b, dest = swap(i)
-        pl.when(jnp.logical_not(home))(lambda s=s, t=t, a=a, b=b, dest=dest: remote(s, t, a, b, dest).wait_send())
-    for cp in sent:
-        cp.wait_send()
+    go_on(gd, gd)
+    if STAGE <= 8:
+        out_ref[...] = res_ref[...]
+        close(normed, *parts)
+        return
+    parts += project(act[...], bufd, FFC, sbuf, fbuf, f_ss, f_rs)
+    for i in range(NX):
+        at = slice(i * 512, (i + 1) * 512)
+        out_ref[:, at] = (hid[:, at].astype(F32) + total(i, fbuf, f_ss, f_rs))[:TOK].astype(BF16)
+    close(normed, *parts)
 
 
 def per_device(
@@ -368,7 +471,7 @@
     first = (blk // 2 * 2 + uly % 2) * 96
     mine = lax.dynamic_slice_in_dim(positions, first, 96).reshape(8, TOK)
     tq = jnp.maximum(jnp.pad(mine, ((0, 0), (0, PAD - TOK))), prefix_len[0] - 1).reshape(8 * PAD, 1)
-    posk = positions.reshape(8, 1, CHUNK)
+    posk = positions.reshape(NX, NY, CHUNK // NX).transpose(1, 0, 2).reshape(NY, 1, CHUNK)
     vm = pl.BlockSpec(memory_space=pltpu.VMEM)
     dma = pltpu.SemaphoreType.DMA
     half = lambda r, w: pltpu.VMEM((NX, NY, 2, r, w), BF16)
@@ -392,20 +495,23 @@
             pltpu.VMEM((GROUP, 8 * PAD, 1), F32),
             pltpu.VMEM((GROUP, 8 * PAD, HEAD_SIZE), F32),
             pltpu.VMEM((8 * PAD, GROUP * HEAD_SIZE), BF16),
-            pltpu.VMEM((8, PAD, D), BF16),
-            pltpu.VMEM((8, PAD, D), BF16),
+            pltpu.VMEM((8, PAD, 1536), BF16),
+            pltpu.VMEM((8, PAD, 1536), BF16),
+            pltpu.VMEM((8, PAD, 1536), BF16),
+            pltpu.VMEM((8, PAD, 1536), BF16),
             pltpu.VMEM((PAD, D), BF16),
-            pltpu.VMEM((PAD, D), BF16),
-            pltpu.VMEM((8, PAD, D), BF16),
+            pltpu.VMEM((PAD, 1536), BF16),
+            pltpu.VMEM((8, PAD, 1536), BF16),
+            pltpu.VMEM((8 * PAD, D), BF16),
             pltpu.VMEM((8 * PAD, FFC), BF16),
             dma((4, 8)), dma((4, 8)),
             dma((4,)), dma((4,)),
             dma((6, 2, 2)), dma((6, 2, 2)),
             dma((6, 2, 4)), dma((6, 2, 4)),
             dma((6, 8)), dma((6, 8)),
+            dma((4, 8)), dma((4, 8)),
             dma((8,)), dma((8,)),
-            dma((8,)), dma((8,)),
-            dma((8,)), dma((8,)),
+            dma((4, 8)), dma((4, 8)),
         ],
         compiler_params=pltpu.CompilerParams(
             collective_id=0, has_side_effects=True, vmem_limit_bytes=60 * 2**20

time: 142 us -> 105 us (0.74)
  Pallas kernels: 138 us -> 100 us
    pallas_call x1, Pallas kernels: 138 us -> 100 us  [per_device(): pl.pallas_call(kernel, out_shape=jax.ShapeDtypeStruct((TOK, D), BF16), in...]
where the time goes in v2:
time: 105 us; the launch traced here: 104 us
  Pallas kernels  100 us (95%)
  local copies, waits for them, and re-layouts  3.24 us (3%)
    pallas_call x1, Pallas kernels, per_device(): pl.pallas_call(kernel, out_shape=jax.ShapeDtypeStruct((TOK, D), BF16), in...  100 us

profile of v2, /device:TPU:1, one launch (start us, length us, event | category | flops | bytes accessed | tf_op | source)
XLA Modules:
  0.0 103.9 jit_solution(7443928091610424289)
XLA Ops:
  0.0 0.0 copy-start
  0.7 0.1 copy-done
  0.8 0.1 dynamic_slice.3
  0.8 0.1 reshape.17
  0.9 0.1 reshape.19
  1.0 0.7 reshape.20.posk_ref
  1.7 0.7 reshape.22.tq_ref
  2.4 100.0 %layer.1 = bf16[12,2048]{1,0:T(8,128)(2,1)} custom-call(bf16[12,4096]{1,0:T(8,128)(2,1)} %q_ref.1, bf16[12,1024]{1,0:T(8,128)(2,1)} %k_ref.1, bf16[12,1024]{1,0:T(8,128)(2,1)} %v_ref.1, bf16[12,4096]{1,0:T(8,128)(2,1)} %g_ref.1, bf16[12,2048]{1,0:T(8,128)(2,1)} %res_ref.1, s32[128,1]{1,0:T(8,128)} %reshape.22.tq_ref, s32[8,1,768]{2,1,0:T(1,128)} %reshape.20.posk_ref, ...), custom_call_target="tpu_custom_call" | custom-call | tf_op jit(solution)/shard_map/layer/pallas_call | solution.py:478
  102.4 1.5 %copy.18 = bf16[12,2048]{1,0:T(8,128)(2,1)} copy(bf16[12,2048]{1,0:T(8,128)(2,1)} %layer.1) | data formatting | bytes 98304
  (2 shorter events, 0.0 us)
Async XLA Ops:
  0.0 0.8 copy-start

commit v3 on v2

--- a/solution.py
+++ b/solution.py
@@ -103,10 +103,10 @@
 
 
 def kernel(
-    q_ref, k_ref, v_ref, g_ref, res_ref, tq_ref, posk_ref, gain_ref, wo_ref, wg_ref, wu_ref, wd_ref,
+    q_ref, k_ref, v_ref, g_ref, res_ref, tq_ref, posa_ref, posb_ref, gain_ref, wo_ref, wg_ref, wu_ref, wd_ref,
     out_ref,
     q16, k16, v16, g16, krec, vrec, qrec, grec, cmp_buf,
-    bufk, bufv, bufo, bufg, bufu, bufd,
+    bufk, bufo, bufg, bufu, bufd,
     m_sc, l_sc, acc, gated, pbuf, rbuf, sbuf, fbuf, hid, nrm, nbuf, rows, act,
     a_ss, a_rs, w_ss, w_rs, x_ss, x_rs, y_ss, y_rs, c_ss, c_rs, r_ss, r_rs, n_ss, n_rs, f_ss, f_rs,
 ):
@@ -120,11 +120,6 @@
 
     home = zh == c
 
-    q16[0:TOK, :] = q_ref[...]
-    k16[0:TOK, :] = k_ref[...]
-    v16[0:TOK, :] = v_ref[...]
-    g16[0:TOK, :] = g_ref[...]
-    hid[0:TOK, :] = res_ref[...]
 
     def out_peer(d):
         z2 = lax.rem(z + d, 8)
@@ -157,6 +152,11 @@
             pl.when(jnp.logical_not(home))(both)
         else:
             both()
+    q16[0:TOK, :] = q_ref[...]
+    k16[0:TOK, :] = k_ref[...]
+    v16[0:TOK, :] = v_ref[...]
+    g16[0:TOK, :] = g_ref[...]
+    hid[0:TOK, :] = res_ref[...]
     pl.when(home)(lambda: pl.semaphore_wait(barrier, 20))
     pl.when(jnp.logical_not(home))(lambda: pl.semaphore_wait(barrier, 22))
 
@@ -201,9 +201,6 @@
         spread(cols(q16, GROUP * HEAD_SIZE), qrec, a_ss.at[2], a_rs.at[2]),
         spread(cols(g16, GROUP * HEAD_SIZE), grec, a_ss.at[3], a_rs.at[3]),
     ]
-    send_all(moves[0])
-    send_all(moves[1])
-
     weights = [(wo_ref, bufo), (wg_ref, bufg), (wu_ref, bufu), (wd_ref, bufd)]
     twin = dev(x, y, c, zl, zh)
 
@@ -211,8 +208,8 @@
         src, buf = weights[i]
         return src, buf.at[x, y, zh], w_ss.at[i], w_rs.at[i], twin
 
-    def swap_start():
-        for i in range(4):
+    def swap_start(first, last):
+        for i in range(first, last):
             s, t, a, b, dest = swap(i)
             pl.when(home)(lambda s=s, t=t, b=b: pltpu.make_async_copy(s, t, b).start())
             pl.when(jnp.logical_not(home))(lambda s=s, t=t, a=a, b=b, dest=dest: remote(s, t, a, b, dest).start())
@@ -221,7 +218,10 @@
         own = weights[i][1].at[x, y, c]
         remote(own, own, w_ss.at[i], w_rs.at[i], other).wait_recv()
 
-    swap_start()
+    swap_start(0, 1)
+    send_all(moves[0])
+    send_all(moves[1])
+    swap_start(1, 4)
     send_all(moves[2])
     send_all(moves[3])
 
@@ -236,16 +236,15 @@
 
     sent = []
 
-    def gather(buf, idx, x_first, rows, theirs_too=True):
+    def gather(buf, idx, x_first, at=(), halves=None, theirs_too=True):
         rx = dict(n=NX, me=x, to=xto, ss=x_ss.at[idx], rs=x_rs.at[idx], log=sent)
         ry = dict(n=NY, me=y, to=yto, ss=y_ss.at[idx], rs=y_rs.at[idx], log=sent)
-        hr = rows // 2
         if x_first:
-            one = Direct(lambda i: buf.at[i, y, c], **rx)
-            two = Ring(lambda i: buf.at[:, i, c], lambda i, w: buf.at[pl.ds(w * 2, 2), i, c], **ry)
+            one = Direct(lambda i: buf.at[(i, y, c) + at], **rx)
+            two = Ring(lambda i: buf.at[(slice(None), i, c) + at], lambda i, w: buf.at[(pl.ds(w * 2, 2), i, c) + at], **ry)
         else:
-            one = Ring(lambda i: buf.at[x, i, c], lambda i, w: buf.at[x, i, c, pl.ds(w * hr, hr)], **ry)
-            two = Ring(lambda i: buf.at[i, :, c], lambda i, w: buf.at[i, pl.ds(w * 4, 4), c], **rx)
+            one = Ring(lambda i: buf.at[(x, i, c) + at], lambda i, w: buf.at[(x, i, c) + halves(w)], **ry)
+            two = Ring(lambda i: buf.at[(i, slice(None), c) + at], lambda i, w: buf.at[(i, pl.ds(w * 4, 4), c) + at], **rx)
 
         def give(j, t):
             cp = remote(two.get(j), two.get(j), c_ss.at[idx, t], c_rs.at[idx, t], other)
@@ -272,7 +271,7 @@
         yield
         if theirs_too:
             for t in range(two.n):
-                theirs(buf, idx, x_first, t)
+                theirs(buf, idx, x_first, t, at)
         yield
 
     def place(n, t):
@@ -280,100 +279,113 @@
             return n // 2
         return -((t + 1) // 2) if t % 2 else t // 2
 
-    def theirs(buf, idx, x_first, t):
+    def spot(x_first, t):
         if x_first:
-            ref = buf.at[:, lax.rem(y + NY + place(NY, t), NY), 1 - c]
-        else:
-            ref = buf.at[lax.rem(x + NX + place(NX, t), NX), :, 1 - c]
+            return lax.rem(y + NY + place(NY, t), NY)
+        return lax.rem(x + NX + place(NX, t), NX)
+
+    def theirs(buf, idx, x_first, t, at):
+        j = spot(x_first, t)
+        ref = buf.at[((slice(None), j) if x_first else (j, slice(None))) + (1 - c,) + at]
         remote(ref, ref, c_ss.at[idx, t], c_rs.at[idx, t], other).wait_recv()
 
-    def compact(rec, buf):
+    def compact(rec, i):
         for s in range(8):
             cmp_buf[TOK * s:TOK * (s + 1), :] = rec[s].astype(F32)[:TOK]
-        buf[x, y, c] = cmp_buf[...].astype(BF16)
-
-    gk = gather(bufk, 0, True, 96, False)
-    gv = gather(bufv, 1, True, 96, False)
-    go = gather(bufo, 2, False, 32)
-    gg = gather(bufg, 3, False, 32)
-    gu = gather(bufu, 4, True, 32)
-    gd = gather(bufd, 5, False, 32)
+        bufk[x, y, c, i] = cmp_buf[...].astype(BF16)
+
+    every = slice(None)
+    k_at = [(every, pl.ds(0, 48)), (every, pl.ds(48, 48))]
+    ka = gather(bufk, 0, True, k_at[0], theirs_too=False)
+    kb = gather(bufk, 1, False, k_at[1], lambda w: (pl.ds(w, 1), pl.ds(48, 48)), theirs_too=False)
+    oa = gather(bufo, 2, True, (pl.ds(0, 16),))
+    ob = gather(bufo, 3, False, (pl.ds(16, 16),), lambda w: (pl.ds(16, 16), pl.ds(w * 256, 256)))
+    gg = gather(bufg, 4, False, (), lambda w: (pl.ds(w * 16, 16),))
+    gu = gather(bufu, 5, True)
+    gd = gather(bufd, 6, False, (), lambda w: (pl.ds(w * 16, 16),))
 
     def go_on(*gens):
         for gen in gens:
             next(gen, None)
 
-    scale = 1.0 / math.sqrt(HEAD_SIZE)
-
-    def attend(first, last):
-        for t in range(first, last):
-            theirs(bufk, 0, True, t)
-            theirs(bufv, 1, True, t)
-
-        def body(i, _):
-            far = lax.div(i + 1, 2)
-            j = lax.rem(y + NY + jnp.where(jnp.logical_and(lax.rem(i, 2) == 1, i < NY - 1), -far, far), NY)
-            keys = bufk[:, j].reshape(CHUNK, HEAD_SIZE)
-            vals = bufv[:, j].reshape(CHUNK, HEAD_SIZE)
-            visible = posk_ref[j] <= tq_ref[...]
-            for g in range(GROUP):
-                q = qrec[:, :, g * HEAD_SIZE:(g + 1) * HEAD_SIZE].reshape(8 * PAD, HEAD_SIZE)
-                s = lax.dot_general(q, keys, (((1,), (1,)), ((), ())), preferred_element_type=F32) * scale
-                s = jnp.where(visible, s, NEG)
-                old = m_sc[g]
-                new = jnp.maximum(old, jnp.max(s, axis=1, keepdims=True))
-                p = jnp.exp(s - new)
-                f = jnp.exp(old - new)
-                l_sc[g] = l_sc[g] * f + jnp.sum(p, axis=1, keepdims=True)
-                acc[g] = acc[g] * f + jnp.dot(p.astype(BF16), vals, preferred_element_type=F32)
-                m_sc[g] = new
-            return 0
-
-        lax.fori_loop(first, last, body, 0)
-
+    power = math.log2(math.e) / math.sqrt(HEAD_SIZE)
+    ones = jnp.ones((CHUNK, HEAD_SIZE), BF16)
+
+    def attend(x_first, *arrivals):
+        keys, vals, pos = [], [], []
+        for t in arrivals:
+            theirs(bufk, 0 if x_first else 1, x_first, t, k_at[0 if x_first else 1])
+        for t in arrivals:
+            j = spot(x_first, t)
+            if x_first:
+                keys.append(bufk[:, j, :, 0, 0:48].reshape(CHUNK // 2, HEAD_SIZE))
+                vals.append(bufk[:, j, :, 1, 0:48].reshape(CHUNK // 2, HEAD_SIZE))
+                pos.append(posa_ref[j])
+            else:
+                keys.append(bufk[j, :, :, 0, 48:96].reshape(CHUNK, HEAD_SIZE))
+                vals.append(bufk[j, :, :, 1, 48:96].reshape(CHUNK, HEAD_SIZE))
+                pos.append(posb_ref[j])
+        join = lambda parts, axis: parts[0] if len(parts) == 1 else jnp.concatenate(parts, axis)
+        keys, vals = join(keys, 0), jnp.concatenate([join(vals, 0), ones], 1)
+        visible = join(pos, 1) <= tq_ref[...]
+        for g in range(GROUP):
+            q = qrec[:, :, g * HEAD_SIZE:(g + 1) * HEAD_SIZE].reshape(8 * PAD, HEAD_SIZE)
+            s = lax.dot_general(q, keys, (((1,), (1,)), ((), ())), preferred_element_type=F32)
+            s = jnp.where(visible, s, NEG)
+            old = m_sc[g]
+            new = jnp.maximum(old, jnp.broadcast_to(jnp.max(s, axis=1, keepdims=True), old.shape))
+            p = jnp.exp2((s - jnp.concatenate([new] * (CHUNK // HEAD_SIZE), 1)) * power)
+            f = jnp.exp2((old - new) * power)
+            o = jnp.dot(p.astype(BF16), vals, preferred_element_type=F32)
+            l_sc[g] = l_sc[g] * f + o[:, HEAD_SIZE:]
+            acc[g] = acc[g] * f + o[:, :HEAD_SIZE]
+            m_sc[g] = new
+
+    swap_wait(0)
+    go_on(oa, ob)
     wait_all_recv(krec, a_ss.at[0], a_rs.at[0])
-    compact(krec, bufk)
-    go_on(gk)
+    compact(krec, 0)
     wait_all_recv(vrec, a_ss.at[1], a_rs.at[1])
-    compact(vrec, bufv)
-    go_on(gv)
+    compact(vrec, 1)
+    go_on(kb, ka)
     m_sc[...] = jnp.full_like(m_sc, NEG)
     l_sc[...] = jnp.zeros_like(l_sc)
     acc[...] = jnp.zeros_like(acc)
-    swap_wait(0)
-    go_on(go)
-    go_on(gk, gv)
-    go_on(go)
+    go_on(ob, kb, ka, oa)
+    go_on(ob, kb)
     for i in range(1, 4):
         swap_wait(i)
-    go_on(gu)
-    go_on(gk, gv)
-    go_on(go)
+    go_on(ka, ob, kb)
+    go_on(oa, ka)
+    go_on(kb, ob)
+    go_on(gg, gu)
     wait_all_recv(qrec, a_ss.at[2], a_rs.at[2])
     wait_all_recv(grec, a_ss.at[3], a_rs.at[3])
-    attend(0, 1)
-    go_on(gk, gv)
-    go_on(go)
+    attend(True, 1, 2)
+    go_on(ka, oa)
+    go_on(gg, gd)
+    attend(False, 0)
+    go_on(kb)
+    attend(True, 3, 4)
+    go_on(ob)
+    go_on(gg, gd)
+    go_on(ka, oa)
+    attend(True, 5, 6)
+    go_on(gg, gd)
+    go_on(gu)
+    attend(False, 1)
+    go_on(kb)
+    attend(False, 2)
     go_on(gg)
-    attend(1, 3)
-    go_on(go)
-    go_on(gk, gv)
+    go_on(oa, ob)
+    attend(True, 0, 7)
     go_on(gd)
-    go_on(gg)
-    go_on(gu)
-    attend(3, 5)
-    go_on(gg, gd)
-    go_on(go)
-    go_on(gk, gv)
-    attend(5, 7)
-    go_on(gg, gd)
-    go_on(go)
-    attend(7, 8)
+    attend(False, 3)
+    go_on(gu, gd)
+    go_on(oa, ob)
     for g in range(GROUP):
         gate = grec[:, :, g * HEAD_SIZE:(g + 1) * HEAD_SIZE].reshape(8 * PAD, HEAD_SIZE).astype(F32)
         gated[:, g * HEAD_SIZE:(g + 1) * HEAD_SIZE] = (acc[g] / l_sc[g] * jax.nn.sigmoid(gate)).astype(BF16)
-    go_on(gg, gd)
-    go_on(go)
     if STAGE <= 4:
         go_on(*[gg, gd, gu] * 9)
         out_ref[...] = res_ref[...]
@@ -412,7 +424,7 @@
 
     parts = project(gated[...], bufo, 512, pbuf, rbuf, r_ss, r_rs)
     go_on(gu)
-    go_on(gd)
+    go_on(gg)
     square = jnp.zeros((PAD, 1), F32)
     for i in range(NX):
         at = slice(i * 512, (i + 1) * 512)
@@ -430,7 +442,6 @@
     go_on(gg)
     go_on(gu)
     go_on(gd)
-    go_on(gg)
     wait_all_recv(nbuf, n_ss, n_rs)
     for i in range(NX):
         at = slice(i * 512, (i + 1) * 512)
@@ -440,7 +451,6 @@
         out_ref[...] = res_ref[...]
         close(normed, *parts)
         return
-    go_on(gu)
     go_on(gg, gu)
     for n in range(FFC // 256):
         at = slice(n * 256, (n + 1) * 256)
@@ -471,14 +481,16 @@
     first = (blk // 2 * 2 + uly % 2) * 96
     mine = lax.dynamic_slice_in_dim(positions, first, 96).reshape(8, TOK)
     tq = jnp.maximum(jnp.pad(mine, ((0, 0), (0, PAD - TOK))), prefix_len[0] - 1).reshape(8 * PAD, 1)
-    posk = positions.reshape(NX, NY, CHUNK // NX).transpose(1, 0, 2).reshape(NY, 1, CHUNK)
+    pos = positions.reshape(NX, NY, 2, 2, 48)
+    posa = pos[:, :, :, 0].transpose(1, 0, 2, 3).reshape(NY, 1, CHUNK // 2)
+    posb = pos[:, :, :, 1].reshape(NX, 1, CHUNK)
     vm = pl.BlockSpec(memory_space=pltpu.VMEM)
     dma = pltpu.SemaphoreType.DMA
     half = lambda r, w: pltpu.VMEM((NX, NY, 2, r, w), BF16)
     return pl.pallas_call(
         kernel,
         out_shape=jax.ShapeDtypeStruct((TOK, D), BF16),
-        in_specs=[vm] * 12,
+        in_specs=[vm] * 13,
         out_specs=vm,
         scratch_shapes=[
             pltpu.VMEM((PAD, 4096), BF16),
@@ -490,9 +502,9 @@
             pltpu.VMEM((8, PAD, 512), BF16),
             pltpu.VMEM((8, PAD, 512), BF16),
             pltpu.VMEM((96, 128), F32),
-            half(96, 128), half(96, 128), half(32, 512), half(32, FFC), half(32, FFC), half(32, FFC),
-            pltpu.VMEM((GROUP, 8 * PAD, 1), F32),
-            pltpu.VMEM((GROUP, 8 * PAD, 1), F32),
+            pltpu.VMEM((NX, NY, 2, 2, 96, 128), BF16), half(32, 512), half(32, FFC), half(32, FFC), half(32, FFC),
+            pltpu.VMEM((GROUP, 8 * PAD, HEAD_SIZE), F32),
+            pltpu.VMEM((GROUP, 8 * PAD, HEAD_SIZE), F32),
             pltpu.VMEM((GROUP, 8 * PAD, HEAD_SIZE), F32),
             pltpu.VMEM((8 * PAD, GROUP * HEAD_SIZE), BF16),
             pltpu.VMEM((8, PAD, 1536), BF16),
@@ -506,9 +518,9 @@
             pltpu.VMEM((8 * PAD, FFC), BF16),
             dma((4, 8)), dma((4, 8)),
             dma((4,)), dma((4,)),
-            dma((6, 2, 2)), dma((6, 2, 2)),
-            dma((6, 2, 4)), dma((6, 2, 4)),
-            dma((6, 8)), dma((6, 8)),
+            dma((7, 2, 2)), dma((7, 2, 2)),
+            dma((7, 2, 4)), dma((7, 2, 4)),
+            dma((7, 8)), dma((7, 8)),
             dma((4, 8)), dma((4, 8)),
             dma((8,)), dma((8,)),
             dma((4, 8)), dma((4, 8)),
@@ -518,7 +530,7 @@
         ),
         name="layer",
     )(
-        query_projection, key_projection, value_projection, gate_proj, residual, tq, posk,
+        query_projection, key_projection, value_projection, gate_proj, residual, tq, posa, posb,
         norm_gain.reshape(1, D), out_weight.T, gate_weight, up_weight, down_weight.T,
     )
 

time: 105 us -> 108 us (1.029)
  Pallas kernels: 100 us -> 103 us
    pallas_call x1, Pallas kernels: 100 us -> 103 us  [per_device(): pl.pallas_call(kernel, out_shape=jax.ShapeDtypeStruct((TOK, D), BF16), in...]
where the time goes in v3:
time: 108 us; the launch traced here: 107 us
  Pallas kernels  103 us (95%)
  local copies, waits for them, and re-layouts  4.15 us (4%)
    pallas_call x1, Pallas kernels, per_device(): pl.pallas_call(kernel, out_shape=jax.ShapeDtypeStruct((TOK, D), BF16), in...  103 us

profile of v3, /device:TPU:1, one launch (start us, length us, event | category | flops | bytes accessed | tf_op | source)
XLA Modules:
  0.0 107.4 jit_solution(4013807415841247839)
XLA Ops:
  0.0 0.0 copy-start
  0.7 0.1 copy-done
  0.8 0.1 dynamic_slice.3
  0.8 0.1 reshape.17
  0.9 0.7 reshape.22.tq_ref
  1.6 0.1 reshape.19
  1.8 0.1 slice_reduce_fusion
  1.9 0.7 reshape_squeeze.3.posb_ref
  2.7 0.7 reshape.20.posa_ref
  3.4 102.6 %layer.1 = bf16[12,2048]{1,0:T(8,128)(2,1)} custom-call(bf16[12,4096]{1,0:T(8,128)(2,1)} %q_ref.1, bf16[12,1024]{1,0:T(8,128)(2,1)} %k_ref.1, bf16[12,1024]{1,0:T(8,128)(2,1)} %v_ref.1, bf16[12,4096]{1,0:T(8,128)(2,1)} %g_ref.1, bf16[12,2048]{1,0:T(8,128)(2,1)} %res_ref.1, s32[128,1]{1,0:T(8,128)} %reshape.22.tq_ref, s32[8,1,384]{2,1,0:T(1,128)} %reshape.20.posa_ref, ...), custom_call_target="tpu_custom_call" | custom-call | tf_op jit(solution)/shard_map/layer/pallas_call | solution.py:490
  106.0 1.5 %copy.19 = bf16[12,2048]{1,0:T(8,128)(2,1)} copy(bf16[12,2048]{1,0:T(8,128)(2,1)} %layer.1) | data formatting | bytes 98304
  (2 shorter events, 0.0 us)
Async XLA Ops:
  0.0 0.8 copy-start

commit v4 on v3

--- a/solution.py
+++ b/solution.py
@@ -20,7 +20,6 @@
 F32 = jnp.float32
 BF16 = jnp.bfloat16
 NEG = -1e30
-STAGE = 99
 
 
 def remote(src, dst, ss, rs, dest):
@@ -160,9 +159,6 @@
     pl.when(home)(lambda: pl.semaphore_wait(barrier, 20))
     pl.when(jnp.logical_not(home))(lambda: pl.semaphore_wait(barrier, 22))
 
-    if STAGE <= 1:
-        out_ref[...] = res_ref[...]
-        return
     order = (4, 3, 5, 2, 6, 1, 7, 0)
 
     def spread(src, dst, ss, rs):
@@ -300,9 +296,13 @@
     kb = gather(bufk, 1, False, k_at[1], lambda w: (pl.ds(w, 1), pl.ds(48, 48)), theirs_too=False)
     oa = gather(bufo, 2, True, (pl.ds(0, 16),))
     ob = gather(bufo, 3, False, (pl.ds(16, 16),), lambda w: (pl.ds(16, 16), pl.ds(w * 256, 256)))
-    gg = gather(bufg, 4, False, (), lambda w: (pl.ds(w * 16, 16),))
-    gu = gather(bufu, 5, True)
-    gd = gather(bufd, 6, False, (), lambda w: (pl.ds(w * 16, 16),))
+    def halved(buf, idx, x_first):
+        split = lambda lo: (lambda w: (pl.ds(lo, 16), pl.ds(w * 384, 384)))
+        return [gather(buf, idx + i, x_first, (pl.ds(16 * i, 16),), split(16 * i)) for i in (0, 1)]
+
+    g1, g2 = halved(bufg, 4, False)
+    u1, u2 = halved(bufu, 6, True)
+    d1, d2 = halved(bufd, 8, False)
 
     def go_on(*gens):
         for gen in gens:
@@ -351,46 +351,43 @@
     m_sc[...] = jnp.full_like(m_sc, NEG)
     l_sc[...] = jnp.zeros_like(l_sc)
     acc[...] = jnp.zeros_like(acc)
+    swap_wait(1)
+    go_on(g1, g2)
     go_on(ob, kb, ka, oa)
-    go_on(ob, kb)
-    for i in range(1, 4):
-        swap_wait(i)
-    go_on(ka, ob, kb)
-    go_on(oa, ka)
-    go_on(kb, ob)
-    go_on(gg, gu)
+    go_on(g1, g2)
+    swap_wait(2)
+    swap_wait(3)
+    go_on(u1, u2)
+    go_on(ob, kb, ka)
+    go_on(g1, g2, d1)
+    go_on(ob, kb, oa, ka)
+    go_on(g1, g2, d1)
+    go_on(kb, ob, g1)
     wait_all_recv(qrec, a_ss.at[2], a_rs.at[2])
     wait_all_recv(grec, a_ss.at[3], a_rs.at[3])
     attend(True, 1, 2)
+    go_on(ka, oa, d1, d2)
+    attend(False, 0)
+    go_on(kb, ob, g2)
+    go_on(u1)
+    attend(True, 3, 4)
+    go_on(d1, d2)
     go_on(ka, oa)
-    go_on(gg, gd)
-    attend(False, 0)
-    go_on(kb)
-    attend(True, 3, 4)
-    go_on(ob)
-    go_on(gg, gd)
-    go_on(ka, oa)
+    go_on(g1)
     attend(True, 5, 6)
-    go_on(gg, gd)
-    go_on(gu)
+    go_on(kb, ob)
+    go_on(d1, u2)
     attend(False, 1)
-    go_on(kb)
+    go_on(oa, d2, u1)
     attend(False, 2)
-    go_on(gg)
-    go_on(oa, ob)
     attend(True, 0, 7)
-    go_on(gd)
+    go_on(g1, g2, d2)
+    go_on(u1, u2)
     attend(False, 3)
-    go_on(gu, gd)
     go_on(oa, ob)
     for g in range(GROUP):
         gate = grec[:, :, g * HEAD_SIZE:(g + 1) * HEAD_SIZE].reshape(8 * PAD, HEAD_SIZE).astype(F32)
         gated[:, g * HEAD_SIZE:(g + 1) * HEAD_SIZE] = (acc[g] / l_sc[g] * jax.nn.sigmoid(gate)).astype(BF16)
-    if STAGE <= 4:
-        go_on(*[gg, gd, gu] * 9)
-        out_ref[...] = res_ref[...]
-        close()
-        return
 
     NT = (((1,), (1,)), ((), ()))
 
@@ -422,9 +419,9 @@
             t = t + into[u, :, at].astype(F32)
         return unpack(t[None])[0]
 
+    go_on(d2, d1)
     parts = project(gated[...], bufo, 512, pbuf, rbuf, r_ss, r_rs)
-    go_on(gu)
-    go_on(gg)
+    go_on(u1, u2, g2, d2, u1, u2)
     square = jnp.zeros((PAD, 1), F32)
     for i in range(NX):
         at = slice(i * 512, (i + 1) * 512)
@@ -438,20 +435,12 @@
         nrm[:, i * 384:(i + 1) * 384] = pack((hid[:, at].astype(F32) * inv * gain_ref[:, at])[None])[0].astype(BF16)
     normed = spread(lambda head: nrm, nbuf, n_ss, n_rs)
     send_all(normed)
-    go_on(gu)
-    go_on(gg)
-    go_on(gu)
-    go_on(gd)
+    go_on(u2, d1, d2)
     wait_all_recv(nbuf, n_ss, n_rs)
     for i in range(NX):
         at = slice(i * 512, (i + 1) * 512)
         rows[:, at] = unpack(nbuf[:, :, i * 384:(i + 1) * 384].astype(F32)).reshape(8 * PAD, 512).astype(BF16)
-    if STAGE <= 7:
-        go_on(*[gg, gd, gu] * 9)
-        out_ref[...] = res_ref[...]
-        close(normed, *parts)
-        return
-    go_on(gg, gu)
+    go_on(g1, g2, u1, u2)
     for n in range(FFC // 256):
         at = slice(n * 256, (n + 1) * 256)
         gate_sum = jnp.zeros((8 * PAD, 256), F32)
@@ -461,11 +450,7 @@
             gate_sum += jnp.dot(r, bufg[i, :, :, :, at].reshape(512, 256), preferred_element_type=F32)
             up_sum += jnp.dot(r, bufu[i, :, :, :, at].reshape(512, 256), preferred_element_type=F32)
         act[:, at] = (jax.nn.silu(gate_sum) * up_sum).astype(BF16)
-    go_on(gd, gd)
-    if STAGE <= 8:
-        out_ref[...] = res_ref[...]
-        close(normed, *parts)
-        return
+    go_on(d1, d2)
     parts += project(act[...], bufd, FFC, sbuf, fbuf, f_ss, f_rs)
     for i in range(NX):
         at = slice(i * 512, (i + 1) * 512)
@@ -518,9 +503,9 @@
             pltpu.VMEM((8 * PAD, FFC), BF16),
             dma((4, 8)), dma((4, 8)),
             dma((4,)), dma((4,)),
-            dma((7, 2, 2)), dma((7, 2, 2)),
-            dma((7, 2, 4)), dma((7, 2, 4)),
-            dma((7, 8)), dma((7, 8)),
+            dma((10, 2, 2)), dma((10, 2, 2)),
+            dma((10, 2, 4)), dma((10, 2, 4)),
+            dma((10, 8)), dma((10, 8)),
             dma((4, 8)), dma((4, 8)),
             dma((8,)), dma((8,)),
             dma((4, 8)), dma((4, 8)),

time: 108 us -> 115 us (1.065)
  Pallas kernels: 103 us -> 109 us
    pallas_call x1, Pallas kernels: 103 us -> 109 us  [per_device(): pl.pallas_call(kernel, out_shape=jax.ShapeDtypeStruct((TOK, D), BF16), in...]
where the time goes in v4:
time: 115 us; the launch traced here: 114 us
  Pallas kernels  109 us (95%)
  local copies, waits for them, and re-layouts  4.15 us (4%)
    pallas_call x1, Pallas kernels, per_device(): pl.pallas_call(kernel, out_shape=jax.ShapeDtypeStruct((TOK, D), BF16), in...  109 us

profile of v4, /device:TPU:1, one launch (start us, length us, event | category | flops | bytes accessed | tf_op | source)
XLA Modules:
  0.0 113.8 jit_solution(18146536985364447055)
XLA Ops:
  0.0 0.0 copy-start
  0.7 0.1 copy-done
  0.8 0.1 dynamic_slice.3
  0.8 0.1 reshape.17
  0.9 0.7 reshape.22.tq_ref
  1.6 0.1 reshape.19
  1.8 0.1 slice_reduce_fusion
  1.9 0.7 reshape_squeeze.3.posb_ref
  2.7 0.7 reshape.20.posa_ref
  3.4 109.0 %layer.1 = bf16[12,2048]{1,0:T(8,128)(2,1)} custom-call(bf16[12,4096]{1,0:T(8,128)(2,1)} %q_ref.1, bf16[12,1024]{1,0:T(8,128)(2,1)} %k_ref.1, bf16[12,1024]{1,0:T(8,128)(2,1)} %v_ref.1, bf16[12,4096]{1,0:T(8,128)(2,1)} %g_ref.1, bf16[12,2048]{1,0:T(8,128)(2,1)} %res_ref.1, s32[128,1]{1,0:T(8,128)} %reshape.22.tq_ref, s32[8,1,384]{2,1,0:T(1,128)} %reshape.20.posa_ref, ...), custom_call_target="tpu_custom_call" | custom-call | tf_op jit(solution)/shard_map/layer/pallas_call | solution.py:475
  112.4 1.5 %copy.19 = bf16[12,2048]{1,0:T(8,128)(2,1)} copy(bf16[12,2048]{1,0:T(8,128)(2,1)} %layer.1) | data formatting | bytes 98304
  (2 shorter events, 0.0 us)
Async XLA Ops:
  0.0 0.8 copy-start

commit v5 on v2

--- a/solution.py
+++ b/solution.py
@@ -20,7 +20,6 @@
 F32 = jnp.float32
 BF16 = jnp.bfloat16
 NEG = -1e30
-STAGE = 99
 
 
 def remote(src, dst, ss, rs, dest):
@@ -120,11 +119,6 @@
 
     home = zh == c
 
-    q16[0:TOK, :] = q_ref[...]
-    k16[0:TOK, :] = k_ref[...]
-    v16[0:TOK, :] = v_ref[...]
-    g16[0:TOK, :] = g_ref[...]
-    hid[0:TOK, :] = res_ref[...]
 
     def out_peer(d):
         z2 = lax.rem(z + d, 8)
@@ -157,12 +151,14 @@
             pl.when(jnp.logical_not(home))(both)
         else:
             both()
+    q16[0:TOK, :] = q_ref[...]
+    k16[0:TOK, :] = k_ref[...]
+    v16[0:TOK, :] = v_ref[...]
+    g16[0:TOK, :] = g_ref[...]
+    hid[0:TOK, :] = res_ref[...]
     pl.when(home)(lambda: pl.semaphore_wait(barrier, 20))
     pl.when(jnp.logical_not(home))(lambda: pl.semaphore_wait(barrier, 22))
 
-    if STAGE <= 1:
-        out_ref[...] = res_ref[...]
-        return
     order = (4, 3, 5, 2, 6, 1, 7, 0)
 
     def spread(src, dst, ss, rs):
@@ -303,7 +299,8 @@
         for gen in gens:
             next(gen, None)
 
-    scale = 1.0 / math.sqrt(HEAD_SIZE)
+    power = math.log2(math.e) / math.sqrt(HEAD_SIZE)
+    ones = jnp.ones((CHUNK, HEAD_SIZE), BF16)
 
     def attend(first, last):
         for t in range(first, last):
@@ -314,18 +311,19 @@
             far = lax.div(i + 1, 2)
             j = lax.rem(y + NY + jnp.where(jnp.logical_and(lax.rem(i, 2) == 1, i < NY - 1), -far, far), NY)
             keys = bufk[:, j].reshape(CHUNK, HEAD_SIZE)
-            vals = bufv[:, j].reshape(CHUNK, HEAD_SIZE)
+            vals = jnp.concatenate([bufv[:, j].reshape(CHUNK, HEAD_SIZE), ones], 1)
             visible = posk_ref[j] <= tq_ref[...]
             for g in range(GROUP):
                 q = qrec[:, :, g * HEAD_SIZE:(g + 1) * HEAD_SIZE].reshape(8 * PAD, HEAD_SIZE)
-                s = lax.dot_general(q, keys, (((1,), (1,)), ((), ())), preferred_element_type=F32) * scale
+                s = lax.dot_general(q, keys, (((1,), (1,)), ((), ())), preferred_element_type=F32)
                 s = jnp.where(visible, s, NEG)
                 old = m_sc[g]
-                new = jnp.maximum(old, jnp.max(s, axis=1, keepdims=True))
-                p = jnp.exp(s - new)
-                f = jnp.exp(old - new)
-                l_sc[g] = l_sc[g] * f + jnp.sum(p, axis=1, keepdims=True)
-                acc[g] = acc[g] * f + jnp.dot(p.astype(BF16), vals, preferred_element_type=F32)
+                new = jnp.maximum(old, jnp.broadcast_to(jnp.max(s, axis=1, keepdims=True), old.shape))
+                p = jnp.exp2((s - jnp.concatenate([new] * (CHUNK // HEAD_SIZE), 1)) * power)
+                f = jnp.exp2((old - new) * power)
+                o = jnp.dot(p.astype(BF16), vals, preferred_element_type=F32)
+                l_sc[g] = l_sc[g] * f + o[:, HEAD_SIZE:]
+                acc[g] = acc[g] * f + o[:, :HEAD_SIZE]
                 m_sc[g] = new
             return 0
 
@@ -348,37 +346,30 @@
         swap_wait(i)
     go_on(gu)
     go_on(gk, gv)
-    go_on(go)
+    go_on(go, gg)
     wait_all_recv(qrec, a_ss.at[2], a_rs.at[2])
     wait_all_recv(grec, a_ss.at[3], a_rs.at[3])
     attend(0, 1)
     go_on(gk, gv)
-    go_on(go)
-    go_on(gg)
+    go_on(go, gg)
     attend(1, 3)
     go_on(go)
     go_on(gk, gv)
-    go_on(gd)
-    go_on(gg)
+    go_on(gg, gd)
     go_on(gu)
     attend(3, 5)
     go_on(gg, gd)
     go_on(go)
+    attend(5, 7)
+    go_on(gg)
     go_on(gk, gv)
-    attend(5, 7)
-    go_on(gg, gd)
-    go_on(go)
+    go_on(go, gd)
     attend(7, 8)
+    go_on(gd)
     for g in range(GROUP):
         gate = grec[:, :, g * HEAD_SIZE:(g + 1) * HEAD_SIZE].reshape(8 * PAD, HEAD_SIZE).astype(F32)
         gated[:, g * HEAD_SIZE:(g + 1) * HEAD_SIZE] = (acc[g] / l_sc[g] * jax.nn.sigmoid(gate)).astype(BF16)
-    go_on(gg, gd)
     go_on(go)
-    if STAGE <= 4:
-        go_on(*[gg, gd, gu] * 9)
-        out_ref[...] = res_ref[...]
-        close()
-        return
 
     NT = (((1,), (1,)), ((), ()))
 
@@ -411,11 +402,11 @@
         return unpack(t[None])[0]
 
     parts = project(gated[...], bufo, 512, pbuf, rbuf, r_ss, r_rs)
-    go_on(gu)
-    go_on(gd)
+    between = [(gu, gg), (gd,), (), (gu,)]
     square = jnp.zeros((PAD, 1), F32)
     for i in range(NX):
         at = slice(i * 512, (i + 1) * 512)
+        go_on(*between[i])
         h = (hid[:, at].astype(F32) + total(i, rbuf, r_ss, r_rs)).astype(BF16)
         hid[:, at] = h
         h = h.astype(F32)
@@ -426,21 +417,14 @@
         nrm[:, i * 384:(i + 1) * 384] = pack((hid[:, at].astype(F32) * inv * gain_ref[:, at])[None])[0].astype(BF16)
     normed = spread(lambda head: nrm, nbuf, n_ss, n_rs)
     send_all(normed)
-    go_on(gu)
     go_on(gg)
     go_on(gu)
     go_on(gd)
-    go_on(gg)
+    go_on(gu)
     wait_all_recv(nbuf, n_ss, n_rs)
     for i in range(NX):
         at = slice(i * 512, (i + 1) * 512)
         rows[:, at] = unpack(nbuf[:, :, i * 384:(i + 1) * 384].astype(F32)).reshape(8 * PAD, 512).astype(BF16)
-    if STAGE <= 7:
-        go_on(*[gg, gd, gu] * 9)
-        out_ref[...] = res_ref[...]
-        close(normed, *parts)
-        return
-    go_on(gu)
     go_on(gg, gu)
     for n in range(FFC // 256):
         at = slice(n * 256, (n + 1) * 256)
@@ -452,10 +436,6 @@
             up_sum += jnp.dot(r, bufu[i, :, :, :, at].reshape(512, 256), preferred_element_type=F32)
         act[:, at] = (jax.nn.silu(gate_sum) * up_sum).astype(BF16)
     go_on(gd, gd)
-    if STAGE <= 8:
-        out_ref[...] = res_ref[...]
-        close(normed, *parts)
-        return
     parts += project(act[...], bufd, FFC, sbuf, fbuf, f_ss, f_rs)
     for i in range(NX):
         at = slice(i * 512, (i + 1) * 512)
@@ -491,8 +471,8 @@
             pltpu.VMEM((8, PAD, 512), BF16),
             pltpu.VMEM((96, 128), F32),
             half(96, 128), half(96, 128), half(32, 512), half(32, FFC), half(32, FFC), half(32, FFC),
-            pltpu.VMEM((GROUP, 8 * PAD, 1), F32),
-            pltpu.VMEM((GROUP, 8 * PAD, 1), F32),
+            pltpu.VMEM((GROUP, 8 * PAD, HEAD_SIZE), F32),
+            pltpu.VMEM((GROUP, 8 * PAD, HEAD_SIZE), F32),
             pltpu.VMEM((GROUP, 8 * PAD, HEAD_SIZE), F32),
             pltpu.VMEM((8 * PAD, GROUP * HEAD_SIZE), BF16),
             pltpu.VMEM((8, PAD, 1536), BF16),

time: 105 us -> 107 us (1.019)
  the two profiles are of different devices: /device:TPU:1 before, /device:TPU:68 now
where the time goes in v5:
time: 107 us
  Pallas kernels  103 us (96%)
  local copies, waits for them, and re-layouts  3.24 us (3%)
    pallas_call x1, Pallas kernels, per_device(): pl.pallas_call(kernel, out_shape=jax.ShapeDtypeStruct((TOK, D), BF16), in...  103 us

profile of v5, /device:TPU:68, one launch (start us, length us, event | category | flops | bytes accessed | tf_op | source)
XLA Modules:
  0.0 106.6 jit_solution(1725813012587800237)
XLA Ops:
  0.0 0.0 copy-start
  0.7 0.1 copy-done
  0.8 0.1 dynamic_slice.3
  0.8 0.1 reshape.17
  0.9 0.1 reshape.19
  1.0 0.7 reshape.20.posk_ref
  1.7 0.7 reshape.22.tq_ref
  2.4 102.7 %layer.1 = bf16[12,2048]{1,0:T(8,128)(2,1)} custom-call(bf16[12,4096]{1,0:T(8,128)(2,1)} %q_ref.1, bf16[12,1024]{1,0:T(8,128)(2,1)} %k_ref.1, bf16[12,1024]{1,0:T(8,128)(2,1)} %v_ref.1, bf16[12,4096]{1,0:T(8,128)(2,1)} %g_ref.1, bf16[12,2048]{1,0:T(8,128)(2,1)} %res_ref.1, s32[128,1]{1,0:T(8,128)} %reshape.22.tq_ref, s32[8,1,768]{2,1,0:T(1,128)} %reshape.20.posk_ref, ...), custom_call_target="tpu_custom_call" | custom-call | tf_op jit(solution)/shard_map/layer/pallas_call | solution.py:458
  105.1 1.5 %copy.18 = bf16[12,2048]{1,0:T(8,128)(2,1)} copy(bf16[12,2048]{1,0:T(8,128)(2,1)} %layer.1) | data formatting | bytes 98304
  (2 shorter events, 0.0 us)
Async XLA Ops:
  0.0 0.8 copy-start
